TPU v7x, 256 devices: a whole 4x4x8 slice. The times are simulated.
256 devices in a mesh: grp: 2 (over z_lo), gx: 64 (over x, z_hi, y), gz: 2 (over core).
Axes of the slice: x: 4, y: 4, z: 8 (z_hi: 4, z_lo: 2; z = z_hi * 2 + z_lo), core: 2. Of those that a mesh axis runs over, the one named last changes fastest.
Arguments:
- fields: float32 [4, 2, 4, 4096, 1024], P(None, 'grp', None, 'gx', 'gz'), may hold values from -4 to 4
- buoyancy: float32 [2, 4, 4096, 1024], P('grp', None, 'gx', 'gz'), may hold values from 0.3 to 0.9
- stiffness: float32 [2, 4, 4096, 1024], P('grp', None, 'gx', 'gz'), may hold values from 0.2 to 0.7
- stress_zero: float32 [4096, 1024], P('gx', 'gz'), may hold values from -5 to 5
- direct_effect: float32 [4096, 1024], P('gx', 'gz'), may hold values from 1 to 8
- log_state: float32 [4096, 1024], P('gx', 'gz'), may hold values from -2 to 2
- kernel: float32 [16, 1024, 4096], P(None, ('grp', 'gx', 'gz')), may hold values from -2 to 2
- history: float32 [16, 1024, 2, 4096], P(None, ('grp', 'gx', 'gz')), may hold values from -5 to 5
- truncation: int32 [1024, 4096], P(('grp', 'gx', 'gz')), may hold values from 1 to 16
Outputs:
- fields_next: float32 [4, 2, 4, 4096, 1024], P(None, 'grp', None, 'gx', 'gz')
- state_next: float32 [4096, 1024], P('gx', 'gz')
- spectra_new: float32 [4, 1024, 2, 4096], P(None, ('grp', 'gx', 'gz'))
All inputs are finite; a program needn't handle non-finite values.
Results may differ from a plain program's by a relative error of at most 0.0003.
Values sent between devices are 32-bit elements; how exact they have to be, the bound alone decides.
A program may use at most 128 MiB of HBM per device.

v0:
```python
import math

import jax
import jax.numpy as jnp
from jax import lax
from jax.sharding import PartitionSpec as P

NSTEP = 4
NEWTON = 4


FACE_NEAR = 9.0 / 8.0
FACE_FAR = 1.0 / 24.0
DAMPING = 1.0
FULL_PRECISION = lax.Precision.HIGHEST


def extended(cells, sides, width):
    for axis, dim in sides:
        count = lax.axis_size(axis)
        ends = count - 1
        head = lax.slice_in_dim(cells, 0, width, axis=dim)
        tail = lax.slice_in_dim(cells, cells.shape[dim] - width, cells.shape[dim], axis=dim)
        cells = jnp.concatenate(
            [
                lax.ppermute(tail, axis, [(i, (i + 1) % count) for i in range(ends)]),
                cells,
                lax.ppermute(head, axis, [((i + 1) % count, i) for i in range(ends)]),
            ],
            axis=dim,
        )
    return cells


def from_partner(x, axis, stride):
    return lax.ppermute(x, axis, [(i, i ^ 1 << stride) for i in range(lax.axis_size(axis))])


def stencil(values, axis_index, pad_before, pad_after):
    widths = [(0, 0)] * values.ndim
    widths[axis_index] = (pad_before, pad_after)
    padded = jnp.pad(values, widths)
    length = values.shape[axis_index]

    def window(offset):
        return lax.slice_in_dim(padded, offset, offset + length, axis=axis_index)

    return FACE_NEAR * (window(2) - window(1)) - FACE_FAR * (window(3) - window(0))


def margin_stencil(padded, axis_index, length, lead_cells):

    def window(offset):
        return lax.slice_in_dim(
            padded, lead_cells + offset, lead_cells + offset + length, axis=axis_index
        )

    return FACE_NEAR * (window(2) - window(1)) - FACE_FAR * (window(3) - window(0))


def inverse_sinh(scaled):
    magnitude = jnp.abs(scaled)
    positive = jnp.log(magnitude + jnp.sqrt(1.0 + magnitude * magnitude))
    return jnp.where(scaled < 0.0, -positive, positive)


def friction(loading, direct_effect, log_state, initial):
    factor = jnp.exp(log_state)
    slip_rate = initial
    for repeat in range(NEWTON):
        scaled = slip_rate * factor
        misfit = direct_effect * inverse_sinh(scaled) + DAMPING * slip_rate - loading
        slope_total = direct_effect * factor / jnp.sqrt(1.0 + scaled * scaled) + DAMPING
        slip_rate = slip_rate - misfit / slope_total
    return slip_rate


def phase_table(first_index, second_index, length, direction):
    turn_count = first_index * second_index % length
    angle_value = turn_count.astype(jnp.float32) * (2.0 * math.pi / length)
    return (jnp.cos(angle_value), direction * jnp.sin(angle_value))


def complex_apply(real_part, imag_part, cos_table, sin_table, formula):
    real_cos = jnp.einsum(formula, real_part, cos_table, precision=FULL_PRECISION)
    imag_sin = jnp.einsum(formula, imag_part, sin_table, precision=FULL_PRECISION)
    real_sin = jnp.einsum(formula, real_part, sin_table, precision=FULL_PRECISION)
    imag_cos = jnp.einsum(formula, imag_part, cos_table, precision=FULL_PRECISION)
    return (real_cos - imag_sin, real_sin + imag_cos)


def strike_forward(values, outer_count, inner_count):
    planes_count = values.shape[0]
    total_count = outer_count * inner_count
    real_part = values[:, 0].reshape(planes_count, outer_count, inner_count)
    imag_part = values[:, 1].reshape(planes_count, outer_count, inner_count)
    outer_iota = jnp.arange(outer_count, dtype=jnp.int32)
    inner_iota = jnp.arange(inner_count, dtype=jnp.int32)
    cos_table, sin_table = phase_table(outer_iota[:, None], outer_iota[None, :], outer_count, -1.0)
    real_part, imag_part = complex_apply(real_part, imag_part, cos_table, sin_table, "rab,ak->rkb")
    cos_table, sin_table = phase_table(outer_iota[:, None], inner_iota[None, :], total_count, -1.0)
    real_part, imag_part = (
        real_part * cos_table - imag_part * sin_table,
        real_part * sin_table + imag_part * cos_table,
    )
    cos_table, sin_table = phase_table(inner_iota[:, None], inner_iota[None, :], inner_count, -1.0)
    real_part, imag_part = complex_apply(real_part, imag_part, cos_table, sin_table, "rkb,bm->rmk")
    return jnp.stack(
        [
            real_part.reshape(planes_count, total_count),
            imag_part.reshape(planes_count, total_count),
        ],
        axis=1,
    )


def strike_inverse(values, outer_count, inner_count):
    planes_count = values.shape[0]
    total_count = outer_count * inner_count
    real_part = values[:, 0].reshape(planes_count, inner_count, outer_count)
    imag_part = values[:, 1].reshape(planes_count, inner_count, outer_count)
    outer_iota = jnp.arange(outer_count, dtype=jnp.int32)
    inner_iota = jnp.arange(inner_count, dtype=jnp.int32)
    cos_table, sin_table = phase_table(inner_iota[:, None], inner_iota[None, :], inner_count, 1.0)
    real_part, imag_part = complex_apply(real_part, imag_part, cos_table, sin_table, "rmk,mb->rkb")
    cos_table, sin_table = phase_table(outer_iota[:, None], inner_iota[None, :], total_count, 1.0)
    real_part, imag_part = (
        real_part * cos_table - imag_part * sin_table,
        real_part * sin_table + imag_part * cos_table,
    )
    cos_table, sin_table = phase_table(outer_iota[:, None], outer_iota[None, :], outer_count, 1.0)
    real_part, imag_part = complex_apply(real_part, imag_part, cos_table, sin_table, "rkb,ka->rab")
    return jnp.stack(
        [
            real_part.reshape(planes_count, total_count),
            imag_part.reshape(planes_count, total_count),
        ],
        axis=1,
    )


def per_device(
    fields, buoyancy, stiffness, stress_zero, direct_effect, log_state, kernel, history, truncation
):
    side_index = lax.axis_index("grp")
    on_plus = side_index == 1
    depth_index = lax.axis_index("gz")
    strike_devices = lax.axis_size("gx")
    depth_devices = lax.axis_size("gz")
    velocity = fields[0]
    normal_stress = fields[1]
    shear_stress = fields[2:4]
    strike_rows = velocity.shape[2]
    depth_cols = velocity.shape[3]
    modes_dev = history.shape[1]
    strike_total = history.shape[3]
    depth_total = depth_cols * depth_devices
    mode_rows = strike_devices * modes_dev
    scale_back = 1.0 / math.sqrt(strike_total * depth_total)
    lag_number = lax.broadcasted_iota(jnp.int32, kernel.shape, 0)
    weights = jnp.where(lag_number < truncation[None], kernel, jnp.zeros_like(kernel))

    def mode_numbers(row_index, depth_part):
        return (
            (side_index * strike_devices + row_index // modes_dev) * depth_devices + depth_part
        ) * modes_dev + row_index % modes_dev

    own_modes = mode_numbers(jnp.arange(mode_rows, dtype=jnp.int32), depth_index)
    depth_iota = jnp.arange(depth_total, dtype=jnp.int32)
    back_cos, back_sin = phase_table(own_modes[:, None], depth_iota[None, :], depth_total, 1.0)
    lagged = history
    spectra = []
    for step_number in range(NSTEP):
        summed = jnp.sum(weights[:, :, None, :] * lagged, axis=0)
        in_space = strike_inverse(summed, strike_devices, strike_rows)
        by_rows = lax.all_to_all(in_space, "gx", split_axis=2, concat_axis=0, tiled=True)
        partial_value = jnp.einsum(
            "jy,jz->yz", by_rows[:, 0], back_cos, precision=FULL_PRECISION
        ) - jnp.einsum("jy,jz->yz", by_rows[:, 1], back_sin, precision=FULL_PRECISION)
        own_depth = lax.psum_scatter(partial_value, "gz", scatter_dimension=1, tiled=True)
        relief = lax.psum(own_depth, "grp") * scale_back
        padded = extended(velocity, (("gx", 2), ("gz", 3)), 2)
        normal_stress = normal_stress + stiffness * stencil(velocity, 1, 2, 1)
        strike_grad = margin_stencil(padded[:, :, :, 2 : 2 + depth_cols], 2, strike_rows, 1)
        depth_grad = margin_stencil(padded[:, :, 2 : 2 + strike_rows, :], 3, depth_cols, 1)
        shear_stress = shear_stress + stiffness * jnp.stack([strike_grad, depth_grad])
        near_plane = velocity[0, 0]
        far_plane = from_partner(near_plane, "grp", 0)
        velocity_plus = jnp.where(on_plus, near_plane, far_plane)
        velocity_minus = jnp.where(on_plus, far_plane, near_plane)
        slip_guess = velocity_plus - velocity_minus
        loading = stress_zero + relief + DAMPING * slip_guess
        slip_rate = friction(loading, direct_effect, log_state, slip_guess)
        traction = loading - DAMPING * slip_rate
        log_state = 0.75 * log_state - 0.2 * jnp.log(1.0 + slip_rate * slip_rate) + 0.1
        normal_stress = normal_stress.at[0, 0].set(jnp.where(on_plus, traction, -traction))
        shear_rim = extended(shear_stress, (("gx", 3), ("gz", 4)), 2)
        strike_div = margin_stencil(shear_rim[0][:, :, :, 2 : 2 + depth_cols], 2, strike_rows, 0)
        depth_div = margin_stencil(shear_rim[1][:, :, 2 : 2 + strike_rows, :], 3, depth_cols, 0)
        velocity = velocity + buoyancy * (stencil(normal_stress, 1, 1, 2) + strike_div + depth_div)
        term_index = jnp.arange(mode_rows * lax.axis_size("gz"), dtype=jnp.int32)
        term_modes = mode_numbers(term_index % mode_rows, term_index // mode_rows)
        depth_here = depth_index * depth_cols + jnp.arange(depth_cols, dtype=jnp.int32)
        cos_part, sin_part = phase_table(
            term_modes[:, None], depth_here[None, :], depth_total, -1.0
        )
        real_term = jnp.einsum("jz,yz->jy", cos_part, slip_rate, precision=FULL_PRECISION)
        imag_term = jnp.einsum("jz,yz->jy", sin_part, slip_rate, precision=FULL_PRECISION)
        by_modes = lax.psum_scatter(
            jnp.stack([real_term, imag_term], axis=1), "gz", scatter_dimension=0, tiled=True
        )
        spread = lax.all_to_all(by_modes, "gx", split_axis=0, concat_axis=2, tiled=True)
        fresh_modes = strike_forward(spread, strike_devices, strike_rows) * scale_back
        spectra.append(fresh_modes)
        lagged = jnp.concatenate([fresh_modes[None], lagged[:-1]], axis=0)
    return (
        jnp.stack([velocity, normal_stress, shear_stress[0], shear_stress[1]]),
        log_state,
        jnp.stack(spectra),
    )


def solution(mesh):
    return jax.shard_map(
        per_device,
        mesh=mesh,
        in_specs=(
            P(None, "grp", None, "gx", "gz"),
            P("grp", None, "gx", "gz"),
            P("grp", None, "gx", "gz"),
            P("gx", "gz"),
            P("gx", "gz"),
            P("gx", "gz"),
            P(None, ("grp", "gx", "gz"), None),
            P(None, ("grp", "gx", "gz"), None, None),
            P(("grp", "gx", "gz"), None),
        ),
        out_specs=(
            P(None, "grp", None, "gx", "gz"),
            P("gx", "gz"),
            P(None, ("grp", "gx", "gz"), None, None),
        ),
        check_vma=False,
    )
```

profile of v0, /device:TPU:1, one launch (start us, length us, event | category | flops | bytes accessed | tf_op | source)
XLA Modules:
  0.0 803.6 jit_solution(6997939394833421156)
XLA Ops:
  26.4 7.4 reshape.589
  33.9 18.6 %all-to-all-start = ((f32[64,1,512]{2,1,0:T(1,128)}), f32[64,1,512]{2,1,0:T(1,128)S(1)}, u32[]{:S(2)}, u32[]{:S(2)}) async-start(f32[64,1,512]{2,1,0:T(1,128)} %reshape.589), calls=%async_computation | async-start | bytes 262144 | tf_op jit(solution)/shard_map/all_to_all | solution.py:176
  69.9 7.9 reshape.590
  94.1 10.1 %collective-permute-start = (f32[64,512]{1,0:T(8,128)}, f32[64,512]{1,0:T(8,128)}, u32[]{:S(2)}, u32[]{:S(2)}) collective-permute-start(f32[64,512]{1,0:T(8,128)} %slice_bitcast_fusion.24), channel_id=1, source_target_pairs={{0,128},{128,0},{1,129},{129,1},{2,130},{130,2},{3,131},{131,3},{4... | collective-permute-start | bytes 393224 | tf_op jit(solution)/shard_map/ppermute | solution.py:36
  117.8 33.4 %all-reduce.13.cloned.1.call-done = f32[64,512]{1,0:T(8,128)} async-done(((f32[64,512]{1,0:T(8,128)}), f32[64,512]{1,0:T(8,128)}) %all-reduce.13.cloned.1.call-update) | async-done | bytes 131088 | tf_op jit(solution)/shard_map/psum | solution.py:181
  187.7 17.2 %all-to-all-start.1 = ((f32[64,1,512]{2,1,0:T(1,128)}), f32[64,1,512]{2,1,0:T(1,128)S(1)}, u32[]{:S(2)}, u32[]{:S(2)}) async-start(f32[64,1,512]{2,1,0:T(1,128)} %reshape.591), calls=%async_computation.3 | async-start | bytes 262144 | tf_op jit(solution)/shard_map/all_to_all | solution.py:212
  208.3 8.1 %all-to-all-done.1 = f32[64,1,512]{2,1,0:T(1,128)S(1)} async-done(((f32[64,1,512]{2,1,0:T(1,128)}), f32[64,1,512]{2,1,0:T(1,128)S(1)}, u32[]{:S(2)}, u32[]{:S(2)}) %all-to-all-start.1) | async-done | bytes 131104 | tf_op jit(solution)/shard_map/all_to_all | solution.py:212
  260.6 7.4 reshape.593
  285.0 8.0 reshape.594
  328.1 32.7 %all-reduce.15.cloned.1.call-done = f32[64,512]{1,0:T(8,128)} async-done(((f32[64,512]{1,0:T(8,128)}), f32[64,512]{1,0:T(8,128)}) %all-reduce.15.cloned.1.call-update) | async-done | bytes 131088 | tf_op jit(solution)/shard_map/psum | solution.py:181
  391.2 7.4 reduce-scatter.15.cloned.1.call-done
  402.2 12.6 %all-to-all-start.3 = ((f32[64,1,512]{2,1,0:T(1,128)}), f32[64,1,512]{2,1,0:T(1,128)}, u32[]{:S(2)}, u32[]{:S(2)}) async-start(f32[64,1,512]{2,1,0:T(1,128)} %reshape.595), calls=%async_computation.7 | async-start | bytes 262144 | tf_op jit(solution)/shard_map/all_to_all | solution.py:212
  418.1 8.6 %all-to-all-done.3 = f32[64,1,512]{2,1,0:T(1,128)} async-done(((f32[64,1,512]{2,1,0:T(1,128)}), f32[64,1,512]{2,1,0:T(1,128)}, u32[]{:S(2)}, u32[]{:S(2)}) %all-to-all-start.3) | async-done | bytes 131104 | tf_op jit(solution)/shard_map/all_to_all | solution.py:212
  454.8 7.5 reshape.597
  480.8 8.3 %reshape.598 = f32[4096,2,4]{2,1,0:T(2,128)} reshape(f32[64,512]{1,0:T(8,128)S(1)} %reduce.44) | data formatting | bytes 262144
  523.7 32.8 %all-reduce.17.cloned.1.call-done = f32[64,512]{1,0:T(8,128)} async-done(((f32[64,512]{1,0:T(8,128)}), f32[64,512]{1,0:T(8,128)}) %all-reduce.17.cloned.1.call-update) | async-done | bytes 131088 | tf_op jit(solution)/shard_map/psum | solution.py:181
  588.4 17.2 %all-to-all-start.5 = ((f32[64,1,512]{2,1,0:T(1,128)}), f32[64,1,512]{2,1,0:T(1,128)S(1)}, u32[]{:S(2)}, u32[]{:S(2)}) async-start(f32[64,1,512]{2,1,0:T(1,128)} %reshape.599), calls=%async_computation.11 | async-start | bytes 262144 | tf_op jit(solution)/shard_map/all_to_all | solution.py:212
  639.7 7.5 reshape.601
  647.2 6.9 all-to-all-start.6
  656.8 8.7 %all-to-all-done.6 = f32[64,1,512]{2,1,0:T(1,128)S(1)} async-done(((f32[64,1,512]{2,1,0:T(1,128)}), f32[64,1,512]{2,1,0:T(1,128)S(1)}, u32[]{:S(2)}, u32[]{:S(2)}) %all-to-all-start.6) | async-done | bytes 131104 | tf_op jit(solution)/shard_map/all_to_all | solution.py:176
  666.5 7.9 reshape.602
  709.1 25.8 %all-reduce.19.cloned.1.call-done = f32[64,512]{1,0:T(8,128)} async-done(((f32[64,512]{1,0:T(8,128)}), f32[64,512]{1,0:T(8,128)}) %all-reduce.19.cloned.1.call-update) | async-done | bytes 131088 | tf_op jit(solution)/shard_map/psum | solution.py:181
  750.1 12.4 %reduce-scatter.23.cloned.1.call-done = f32[256,2,64]{0,2,1:T(8,128)} async-done(((f32[512,2,64]{0,2,1:T(8,128)}), f32[256,2,64]{0,2,1:T(8,128)}) %reduce-scatter.23.cloned.1.call-update) | async-done | bytes 131088 | tf_op jit(solution)/shard_map/reduce_scatter | solution.py:209
  764.5 12.3 %all-to-all-start.7 = ((f32[64,1,512]{2,1,0:T(1,128)}), f32[64,1,512]{2,1,0:T(1,128)S(1)}, u32[]{:S(2)}, u32[]{:S(2)}) async-start(f32[64,1,512]{2,1,0:T(1,128)} %reshape.603), calls=%async_computation.15 | async-start | bytes 262144 | tf_op jit(solution)/shard_map/all_to_all | solution.py:212
  (453 shorter events, 460.5 us)
Async XLA Ops:
  8.4 44.1 %collective-permute-start.1 = (f32[1,4,2,512]{3,2,1,0:T(2,128)S(1)}, f32[1,4,2,512]{3,2,1,0:T(2,128)S(1)}, u32[]{:S(2)}, u32[]{:S(2)}) collective-permute-start(f32[1,4,2,512]{3,2,1,0:T(2,128)S(1)} %get-tuple-element.127), channel_id=1, source_target_pairs={{2,0},{4,2},{6,4},{8,6},{10,8},{12,10},{14,12},{16,14},{18,16},{20... | collective-permute-start | bytes 49160 | tf_op jit(solution)/shard_map/ppermute | solution.py:28
  9.7 42.8 %collective-permute-start.2 = (f32[1,4,2,512]{3,2,1,0:T(2,128)S(1)}, f32[1,4,2,512]{3,2,1,0:T(2,128)S(1)}, u32[]{:S(2)}, u32[]{:S(2)}) collective-permute-start(f32[1,4,2,512]{3,2,1,0:T(2,128)S(1)} %get-tuple-element.126), channel_id=1, source_target_pairs={{0,2},{2,4},{4,6},{6,8},{8,10},{10,12},{12,14},{14,16},{16,18},{18... | collective-permute-start | bytes 49160 | tf_op jit(solution)/shard_map/ppermute | solution.py:26
  33.9 34.6 %all-to-all-start = ((f32[64,1,512]{2,1,0:T(1,128)}), f32[64,1,512]{2,1,0:T(1,128)S(1)}, u32[]{:S(2)}, u32[]{:S(2)}) async-start(f32[64,1,512]{2,1,0:T(1,128)} %reshape.589), calls=%async_computation | async-start | bytes 262144 | tf_op jit(solution)/shard_map/all_to_all | solution.py:176
  52.5 62.6 %reduce-scatter.9.cloned.1.call-start = ((), (), s32[]{:S(2)}) async-start(), calls=%async_computation.16 | async-start | bytes 393216 | tf_op jit(solution)/shard_map/reduce_scatter | solution.py:180
  63.7 40.4 %collective-permute-start.5 = (f32[2,1,4,2,512]{4,3,2,1,0:T(2,128)}, f32[2,1,4,2,512]{4,3,2,1,0:T(2,128)S(1)}, u32[]{:S(2)}, u32[]{:S(2)}) collective-permute-start(f32[2,1,4,2,512]{4,3,2,1,0:T(2,128)} %get-tuple-element.98), channel_id=1, source_target_pairs={{0,2},{2,4},{4,6},{6,8},{8,10},{10,12},{12,14},{14,16},{16,18},{18... | collective-permute-start | bytes 98312 | tf_op jit(solution)/shard_map/ppermute | solution.py:26
  66.9 37.2 %collective-permute-start.6 = (f32[2,1,4,2,512]{4,3,2,1,0:T(2,128)}, f32[2,1,4,2,512]{4,3,2,1,0:T(2,128)S(1)}, u32[]{:S(2)}, u32[]{:S(2)}) collective-permute-start(f32[2,1,4,2,512]{4,3,2,1,0:T(2,128)} %get-tuple-element.99), channel_id=1, source_target_pairs={{2,0},{4,2},{6,4},{8,6},{10,8},{12,10},{14,12},{16,14},{18,16},{20... | collective-permute-start | bytes 98312 | tf_op jit(solution)/shard_map/ppermute | solution.py:28
  93.4 57.8 %all-reduce.13.cloned.1.call-start = ((), (), s32[]{:S(2)}) async-start(), calls=%async_computation.17 | async-start | bytes 262144 | tf_op jit(solution)/shard_map/psum | solution.py:181
  115.2 70.6 %reduce-scatter.11.cloned.1.call-start = ((), (), s32[]{:S(2)}) async-start(), calls=%async_computation.18 | async-start | bytes 393216 | tf_op jit(solution)/shard_map/reduce_scatter | solution.py:209
  272.6 52.8 %reduce-scatter.13.cloned.1.call-start = ((), (), s32[]{:S(2)}) async-start(), calls=%async_computation.19 | async-start | bytes 393216 | tf_op jit(solution)/shard_map/reduce_scatter | solution.py:180
  275.7 32.9 %collective-permute-start.14 = (f32[2,1,4,2,512]{4,3,2,1,0:T(2,128)S(1)}, f32[2,1,4,2,512]{4,3,2,1,0:T(2,128)S(1)}, u32[]{:S(2)}, u32[]{:S(2)}) collective-permute-start(f32[2,1,4,2,512]{4,3,2,1,0:T(2,128)S(1)} %get-tuple-element.96), channel_id=1, source_target_pairs={{0,2},{2,4},{4,6},{6,8},{8,10},{10,12},{12,14},{14,16},{16,18},{18... | collective-permute-start | bytes 98312 | tf_op jit(solution)/shard_map/ppermute | solution.py:26
  278.5 30.1 %collective-permute-start.15 = (f32[2,1,4,2,512]{4,3,2,1,0:T(2,128)S(1)}, f32[2,1,4,2,512]{4,3,2,1,0:T(2,128)S(1)}, u32[]{:S(2)}, u32[]{:S(2)}) collective-permute-start(f32[2,1,4,2,512]{4,3,2,1,0:T(2,128)S(1)} %get-tuple-element.97), channel_id=1, source_target_pairs={{2,0},{4,2},{6,4},{8,6},{10,8},{12,10},{14,12},{16,14},{18,16},{20... | collective-permute-start | bytes 98312 | tf_op jit(solution)/shard_map/ppermute | solution.py:28
  308.5 52.2 %all-reduce.15.cloned.1.call-start = ((), (), s32[]{:S(2)}) async-start(), calls=%async_computation.20 | async-start | bytes 262144 | tf_op jit(solution)/shard_map/psum | solution.py:181
  325.5 73.1 %reduce-scatter.15.cloned.1.call-start = ((), (), s32[]{:S(2)}) async-start(), calls=%async_computation.21 | async-start | bytes 393216 | tf_op jit(solution)/shard_map/reduce_scatter | solution.py:209
  467.7 53.3 %reduce-scatter.17.cloned.1.call-start = ((), (), s32[]{:S(2)}) async-start(), calls=%async_computation.22 | async-start | bytes 393216 | tf_op jit(solution)/shard_map/reduce_scatter | solution.py:180
  471.8 32.9 %collective-permute-start.23 = (f32[2,1,4,2,512]{4,3,2,1,0:T(2,128)}, f32[2,1,4,2,512]{4,3,2,1,0:T(2,128)S(1)}, u32[]{:S(2)}, u32[]{:S(2)}) collective-permute-start(f32[2,1,4,2,512]{4,3,2,1,0:T(2,128)} %get-tuple-element.94), channel_id=1, source_target_pairs={{0,2},{2,4},{4,6},{6,8},{8,10},{10,12},{12,14},{14,16},{16,18},{18... | collective-permute-start | bytes 98312 | tf_op jit(solution)/shard_map/ppermute | solution.py:26
  474.6 30.2 %collective-permute-start.24 = (f32[2,1,4,2,512]{4,3,2,1,0:T(2,128)}, f32[2,1,4,2,512]{4,3,2,1,0:T(2,128)}, u32[]{:S(2)}, u32[]{:S(2)}) collective-permute-start(f32[2,1,4,2,512]{4,3,2,1,0:T(2,128)} %get-tuple-element.95), channel_id=1, source_target_pairs={{2,0},{4,2},{6,4},{8,6},{10,8},{12,10},{14,12},{16,14},{18,16},{20... | collective-permute-start | bytes 98312 | tf_op jit(solution)/shard_map/ppermute | solution.py:28
  504.7 51.8 %all-reduce.17.cloned.1.call-start = ((), (), s32[]{:S(2)}) async-start(), calls=%async_computation.23 | async-start | bytes 262144 | tf_op jit(solution)/shard_map/psum | solution.py:181
  521.1 65.3 %reduce-scatter.19.cloned.1.call-start = ((), (), s32[]{:S(2)}) async-start(), calls=%async_computation.24 | async-start | bytes 393216 | tf_op jit(solution)/shard_map/reduce_scatter | solution.py:209
  609.2 45.0 %collective-permute-start.31 = (f32[1,4,68,2]{3,2,1,0:T(8,128)}, f32[1,4,68,2]{3,2,1,0:T(8,128)}, u32[]{:S(2)}, u32[]{:S(2)}) collective-permute-start(f32[1,4,68,2]{3,2,1,0:T(8,128)} %get-tuple-element.103), channel_id=1, source_target_pairs={{0,1},{2,3},{4,5},{6,7},{8,9},{10,11},{12,13},{14,15},{16,17},{18,... | collective-permute-start | bytes 6536 | tf_op jit(solution)/shard_map/ppermute | solution.py:26
  654.1 45.3 %reduce-scatter.21.cloned.1.call-start = ((), (), s32[]{:S(2)}) async-start(), calls=%async_computation.25 | async-start | bytes 393216 | tf_op jit(solution)/shard_map/reduce_scatter | solution.py:180
  690.0 44.9 %all-reduce.19.cloned.1.call-start = ((), (), s32[]{:S(2)}) async-start(), calls=%async_computation.26 | async-start | bytes 262144 | tf_op jit(solution)/shard_map/psum | solution.py:181
  699.5 63.0 %reduce-scatter.23.cloned.1.call-start = ((), (), s32[]{:S(2)}) async-start(), calls=%async_computation.27 | async-start | bytes 393216 | tf_op jit(solution)/shard_map/reduce_scatter | solution.py:209
  701.2 46.5 %collective-permute-start.34 = (f32[2,1,4,68,2]{4,3,2,1,0:T(8,128)}, f32[2,1,4,68,2]{4,3,2,1,0:T(8,128)S(1)}, u32[]{:S(2)}, u32[]{:S(2)}) collective-permute-start(f32[2,1,4,68,2]{4,3,2,1,0:T(8,128)} %get-tuple-element.84), channel_id=1, source_target_pairs={{0,1},{2,3},{4,5},{6,7},{8,9},{10,11},{12,13},{14,15},{16,17},{18,... | collective-permute-start | bytes 13064 | tf_op jit(solution)/shard_map/ppermute | solution.py:26
  702.5 45.2 %collective-permute-start.35 = (f32[2,1,4,68,2]{4,3,2,1,0:T(8,128)}, f32[2,1,4,68,2]{4,3,2,1,0:T(8,128)S(1)}, u32[]{:S(2)}, u32[]{:S(2)}) collective-permute-start(f32[2,1,4,68,2]{4,3,2,1,0:T(8,128)} %get-tuple-element.85), channel_id=1, source_target_pairs={{1,0},{3,2},{5,4},{7,6},{9,8},{11,10},{13,12},{15,14},{17,16},{19,... | collective-permute-start | bytes 13064 | tf_op jit(solution)/shard_map/ppermute | solution.py:28
  (82 other events, 1418.4 us)
Sparse Core Ops, SparseCore 0:
  93.5 17.6 reduce-scatter.8
  115.3 35.8 all-reduce.12
  164.1 14.6 reduce-scatter.10
  308.6 16.7 reduce-scatter.12
  327.8 32.8 all-reduce.14
  380.1 18.4 reduce-scatter.14
  504.8 16.1 reduce-scatter.16
  523.6 32.8 all-reduce.16
  569.5 14.6 reduce-scatter.18
  690.1 9.2 reduce-scatter.20
  702.0 32.8 all-reduce.18
  747.8 14.6 reduce-scatter.22
where the time goes:
time: 815 us; the launch traced here: 804 us
  waiting for transfers between devices  205 us (25%)
  starting transfers between devices  197 us (24%)
  local copies, waits for them, and re-layouts  159 us (20%)
  matrix products  123 us (15%)
  other arithmetic  104 us (13%)
  between operations  16.4 us (2%)
    psum x4, waiting for transfers between devices, per_device(): relief = lax.psum(own_depth, 'grp') * scale_back  125 us
    unnamed x116, local copies, waits for them, and re-layouts  73.8 us
    all_to_all x4, starting transfers between devices, per_device(): lax.all_to_all(by_modes, 'gx', split_axis=0, concat_axis=2, tiled=True)  59.3 us
    ppermute x16, starting transfers between devices, extended(): lax.ppermute(head, axis, [((i + 1) % count, i) for i in range(ends)])  50.3 us
    ppermute x16, starting transfers between devices, extended(): lax.ppermute(tail, axis, [(i, (i + 1) % count) for i in range(ends)])  38.2 us
    all_to_all x4, starting transfers between devices, per_device(): lax.all_to_all(in_space, 'gx', split_axis=2, concat_axis=0, tiled=True)  35.7 us
    all_to_all x4, waiting for transfers between devices, per_device(): lax.all_to_all(by_modes, 'gx', split_axis=0, concat_axis=2, tiled=True)  27.6 us
    all_to_all x9, local copies, waits for them, and re-layouts, per_device(): lax.all_to_all(in_space, 'gx', split_axis=2, concat_axis=0, tiled=True)  22.7 us
  transfers between devices with their start and end apart: 56, of which 22 were waited for; matrix products, arithmetic and copies ran while one was open for 28% of the time, Pallas kernels for 0%

commit v1 on v0

v1 whole, which is shorter than its diff:
```python
import functools
import math

import jax
import jax.numpy as jnp
import numpy as np
from jax import lax
from jax.experimental import pallas as pl
from jax.experimental.pallas import tpu as pltpu
from jax.sharding import PartitionSpec as P

NSTEP = 4
NEWTON = 4
C1 = 9.0 / 8.0
C2 = 1.0 / 24.0
MESH = pl.DeviceIdType.MESH
BF = jnp.bfloat16
F32 = jnp.float32


def split_table(table):
    hi = np.asarray(table, np.float32).astype(jnp.bfloat16)
    lo = (table - hi.astype(np.float64)).astype(jnp.bfloat16)
    return np.stack([hi, lo])


def cis(turns):
    return np.cos(2 * np.pi * turns), np.sin(2 * np.pi * turns)


def make_tables(nx, rows, modes, scale):
    A = 2 * nx
    B = rows // 2
    R = modes
    depth = 4 * nx * R
    strike = nx * rows
    eye_r = np.eye(R)
    eye_p = np.eye(2)
    m, b, k, a = np.arange(B), np.arange(B), np.arange(A), np.arange(A)
    c, s = cis(np.outer(m, b) / B)
    inv = np.array([[c, -s], [s, c]])
    fwd = np.array([[c, s], [-s, c]])
    L1 = np.einsum("xybm,rs->xrbysm", inv, eye_r).reshape(2 * R * B, 2 * R * B)
    L3 = np.einsum("xymb,rs->xrmysb", fwd, eye_r).reshape(2 * R * B, 2 * R * B) * scale
    c, s = cis(np.outer(b, k) / strike)
    twiddle = np.stack([np.tile(c, (R, 1)), np.tile(s, (R, 1))])
    c, s = cis(np.outer(a, k) / A)
    inv = np.array([[c, -s], [s, c]]).reshape(2, 2, nx, 2, A)
    T2 = np.einsum("xyjpk->jxpyk", inv).reshape(4 * nx, 2 * A)
    fwd = np.array([[c, s], [-s, c]]).reshape(2, 2, nx, 2, A)
    TV = np.einsum("xyjpk->jpyxk", fwd).reshape(4 * nx, 2 * A)
    i, z = np.arange(nx), np.arange(A)
    c, s = cis(np.outer(i, z) / A)
    sign = np.where(np.arange(2)[:, None] * z[None, :] % 2 == 1, -1.0, 1.0)
    inv = np.array([[c, -s], [s, c]])
    TI = np.einsum("xyiz,gz,pn->giypnxz", inv, sign, eye_p).reshape(8 * nx, 4 * A)
    fwd = np.array([[c, s], [-s, c]])
    TF = np.einsum("xyiz,pn->ipxnyz", fwd, eye_p).reshape(4 * nx, 4 * A)
    zz = np.arange(depth).reshape(2 * R, 1, A)
    r = np.arange(R)[None, :, None]
    wi, wf = [], []
    for q in range(2):
        c, s = cis((R * q + r) * zz / depth)
        wi.append(np.stack([c, -s], axis=2).reshape(2 * R, 2 * R, A) * scale)
    for g in range(2):
        for q in range(2):
            c, s = cis((R * q + r) * zz / depth)
            wf.append(np.stack([c, -s], axis=2).reshape(2 * R, 2 * R, A) * sign[g])
    mats = [split_table(x) for x in (L1, T2, TI, TF, TV, L3)]
    return mats, [np.asarray(x, np.float32) for x in (twiddle, np.stack(wi), np.stack(wf))]


def split(x):
    hi = x.astype(BF)
    return hi, (x - hi.astype(F32)).astype(BF)


def dot(x, y, dims):
    return lax.dot_general(x, y, (dims, ((), ())), preferred_element_type=F32)


def table_left(tab, x, dims):
    hi, lo = split(x)
    return dot(tab[0], hi, dims) + (dot(tab[0], lo, dims) + dot(tab[1], hi, dims))


def table_right(x, tab, dims):
    hi, lo = split(x)
    return dot(hi, tab[0], dims) + (dot(lo, tab[0], dims) + dot(hi, tab[1], dims))


def roll(x, shift, axis):
    return pltpu.roll(x, shift % x.shape[axis], axis)


def kernel_body(
    nx, both, fields, buoy, stiff, szero, direct, logs, start, wts, L1, T2, TI, TF, TV, L3, TW, WI, WF,
    out_f, out_l, out_s,
    VP, SP, DP, ACC, GS, RI, OS, PS, RL, PR, SL, US, SF, RF, TR, SG, HV, DV, NP, HS, DS,
    isend, irecv, fsend, frecv, psend, precv, lsend, lrecv, vsend, vrecv, ssend, srecv, gsend, grecv,
):
    g, j, q = lax.axis_index("grp"), lax.axis_index("gx"), lax.axis_index("gz")
    A = 2 * nx
    RB = TW.shape[1]
    RW, CW = szero.shape
    B = RW // 2
    R = RB // B
    LW = DV.shape[3]
    HC = CW // A
    side = (2 * g - 1).astype(F32)
    rows_in = pl.ds(8, RW)
    cols_in = pl.ds(LW, CW)

    def target(step):
        if nx == 64:
            dx, dz, dy = step // 4 % 4, step // 16, step % 4
            x = lax.rem(j // 16 + (6 - dx), 4)
            z = lax.rem(j // 4 % 4 + (6 - dz), 4)
            y = lax.rem(j % 4 + (6 - dy), 4)
            return x * 16 + z * 4 + y
        return lax.rem(j + step, nx)

    own_step = 2 * 16 + 2 * 4 + 2 if nx == 64 else 0

    barrier = pltpu.get_barrier_semaphore()

    def greet(step, carry):
        peer = target(step)

        @pl.when(step != own_step)
        def _():
            pl.semaphore_signal(barrier, inc=1, device_id=(g, peer, q), device_id_type=MESH)
            if both:
                pl.semaphore_signal(barrier, inc=1, device_id=(1 - g, peer, q), device_id_type=MESH)

        return carry

    lax.fori_loop(0, nx, greet, 0)
    pl.semaphore_signal(barrier, inc=1, device_id=(1 - g, j, q), device_id_type=MESH)
    pl.semaphore_signal(barrier, inc=1, device_id=(g, j, 1 - q), device_id_type=MESH)

    VP[...] = jnp.zeros_like(VP)
    SP[...] = jnp.zeros_like(SP)
    DP[...] = jnp.zeros_like(DP)
    VP[:, rows_in, cols_in] = fields[0]
    out_f[1] = fields[1]
    SP[:, rows_in, :] = fields[2]
    DP[:, :, cols_in] = fields[3]
    out_l[...] = logs[...]
    ACC[pl.ds(0, NSTEP)] = start[...]
    for t in range(NSTEP, ACC.shape[0]):
        ACC[t] = jnp.zeros_like(ACC[t])
    pl.semaphore_wait(barrier, (2 * (nx - 1) if both else nx - 1) + 2)

    def remote(src, dst, send, recv, device):
        return pltpu.make_async_remote_copy(
            src_ref=src, dst_ref=dst, send_sem=send, recv_sem=recv, device_id=device, device_id_type=MESH
        )

    def row_copies(src_of, land, t, send, recv):
        up = remote(src_of(pl.ds(RW, 8)), land.at[t, 0], send.at[0], recv.at[0, t], (g, lax.rem(j + 1, nx), q))
        down = remote(src_of(pl.ds(8, 8)), land.at[t, 1], send.at[1], recv.at[1, t], (g, lax.rem(j + nx - 1, nx), q))
        return up, down

    def v_copies(t):
        up, down = row_copies(lambda d: VP.at[:, d, cols_in], HV, t, vsend, vrecv)
        right = remote(VP.at[:, rows_in, pl.ds(CW, LW)], DV.at[t], vsend.at[2], vrecv.at[2, t], (g, j, 1 - q))
        left = remote(VP.at[:, rows_in, pl.ds(LW, LW)], DV.at[t], vsend.at[2], vrecv.at[2, t], (g, j, 1 - q))
        across = remote(VP.at[0, rows_in, cols_in], NP.at[t], gsend, grecv.at[t], (1 - g, j, q))
        return up, down, right, left, across

    def s_copies(t):
        up, down = row_copies(lambda d: SP.at[:, d, :], HS, t, ssend, srecv)
        right = remote(DP.at[:, :, pl.ds(CW, LW)], DS.at[t], ssend.at[2], srecv.at[2, t], (g, j, 1 - q))
        left = remote(DP.at[:, :, pl.ds(LW, LW)], DS.at[t], ssend.at[2], srecv.at[2, t], (g, j, 1 - q))
        return up, down, right, left

    def start_halo(up, down, right, left):
        @pl.when(j < nx - 1)
        def _():
            up.start()

        @pl.when(j > 0)
        def _():
            down.start()

        @pl.when(q == 0)
        def _():
            right.start()

        @pl.when(q == 1)
        def _():
            left.start()

    def sent_halo(up, down, right, left):
        @pl.when(j < nx - 1)
        def _():
            up.wait_send()

        @pl.when(j > 0)
        def _():
            down.wait_send()

        right.wait_send()

    def recv_halo(up, down, right, t, land, depth_land, put_rows, put_cols):
        @pl.when(j > 0)
        def _():
            up.wait_recv()
            put_rows(0, land[t, 0])

        @pl.when(j < nx - 1)
        def _():
            down.wait_recv()
            put_rows(8 + RW, land[t, 1])

        right.wait_recv()

        @pl.when(q == 0)
        def _():
            put_cols(LW + CW, depth_land[t])

        @pl.when(q == 1)
        def _():
            put_cols(0, depth_land[t])

    def v_rows(at, x):
        VP[:, pl.ds(at, 8), cols_in] = x

    def v_cols(at, x):
        VP[:, rows_in, pl.ds(at, LW)] = x

    def s_rows(at, x):
        SP[:, pl.ds(at, 8), :] = x

    def d_cols(at, x):
        DP[:, :, pl.ds(at, LW)] = x

    first = v_copies(0)
    start_halo(*first[:4])
    first[4].start()

    def step_body(t, carry):
        x = table_left(L1, ACC[t], ((1,), (0,)))
        xr, xi = x[:RB], x[RB:]
        wide = jnp.concatenate([xr * TW[0] - xi * TW[1], xr * TW[1] + xi * TW[0]], axis=1)
        GS[t] = table_left(T2, wide, ((1,), (1,)))
        mine = pl.ds((g * nx + j) * 4, 4)

        def send_modes(step, c):
            peer = target(step)
            block = GS.at[t, pl.ds(peer * 4, 4)]

            @pl.when(step != own_step)
            def _():
                remote(block, RI.at[t, mine], isend.at[t], irecv.at[t], (g, peer, q)).start()
                if both:
                    remote(block, RI.at[t, mine], isend.at[t], irecv.at[t], (1 - g, peer, q)).start()

            return c

        lax.fori_loop(0, nx, send_modes, 0)
        own = GS.at[t, pl.ds(j * 4, 4)]
        pltpu.make_async_copy(own, RI.at[t, mine], irecv.at[t]).start()
        if both:
            remote(own, RI.at[t, mine], isend.at[t], irecv.at[t], (1 - g, j, q)).start()

        up, down, right, left, across = v_copies(t)
        recv_halo(up, down, right, t, HV, DV, v_rows, v_cols)
        sent_halo(up, down, right, left)
        across.wait()
        near = VP[0, rows_in, cols_in]
        SG[...] = side * (near - NP[t])

        def stress_chunk(i, c):
            r0 = pl.multiple_of(i * 8, 8)
            chunk = pl.ds(r0, 8)
            inner = pl.ds(r0 + 8, 8)
            vs = []
            for p in range(4):
                tall = VP[p, pl.ds(r0, 24), cols_in]
                wide = VP[p, inner, :]
                v = tall[8:16]
                vs.append(v)
                st = stiff[p, chunk, :]
                up1, up2, dn1 = (roll(tall, s, 0)[8:16] for s in (-1, -2, 1))
                SP[p, inner, :] = SP[p, inner, :] + st * (C1 * (up1 - v) - C2 * (up2 - dn1))
                up1, up2, dn1 = (roll(wide, s, 1)[:, LW : LW + CW] for s in (-1, -2, 1))
                DP[p, chunk, cols_in] = DP[p, chunk, cols_in] + st * (C1 * (up1 - v) - C2 * (up2 - dn1))
            for p in range(1, 4):
                far = 0.0 - (vs[p - 2] if p >= 2 else 0.0)
                if p < 3:
                    far = vs[p + 1] + far
                out_f[1, p, chunk, :] = out_f[1, p, chunk, :] + stiff[p, chunk, :] * (
                    C1 * (vs[p] - vs[p - 1]) - C2 * far
                )
            return c

        lax.fori_loop(0, RW // 8, stress_chunk, 0)
        up, down, right, left = s_copies(t)
        start_halo(up, down, right, left)
        recv_halo(up, down, right, t, HS, DS, s_rows, d_cols)
        sent_halo(up, down, right, left)

        def velocity_chunk(i, c):
            r0 = pl.multiple_of(i * 8, 8)
            chunk = pl.ds(r0, 8)
            inner = pl.ds(r0 + 8, 8)
            n1, n2, n3 = (out_f[1, p, chunk, :] for p in (1, 2, 3))
            plane_terms = [C1 * n1 - C2 * n2, C1 * (n2 - n1) - C2 * n3, C1 * (n3 - n2) + C2 * n1, C2 * n2 - C1 * n3]
            for p in range(4):
                tall = SP[p, pl.ds(r0, 24), :]
                wide = DP[p, chunk, :]
                dn1, dn2, up1 = (roll(tall, s, 0)[8:16] for s in (1, 2, -1))
                total = plane_terms[p] + (C1 * (tall[8:16] - dn1) - C2 * (up1 - dn2))
                dn1, dn2, up1 = (roll(wide, s, 1)[:, LW : LW + CW] for s in (1, 2, -1))
                total = total + (C1 * (wide[:, LW : LW + CW] - dn1) - C2 * (up1 - dn2))
                VP[p, inner, cols_in] = VP[p, inner, cols_in] + buoy[p, chunk, :] * total
            return c

        lax.fori_loop(0, RW // 8, velocity_chunk, 0)

        if not both:
            pltpu.make_async_copy(
                RI.at[t, pl.ds(g * nx * 4, nx * 4)], RI.at[t, pl.ds(g * nx * 4, nx * 4)], irecv.at[t]
            ).wait()
            relay = remote(
                RI.at[t, pl.ds(g * nx * 4, nx * 4)], RI.at[t, pl.ds(g * nx * 4, nx * 4)], psend.at[1, t],
                precv.at[1, t], (1 - g, j, q),
            )
            relay.start()
            relay.wait()
        else:
            pltpu.make_async_copy(RI.at[t], RI.at[t], irecv.at[t]).wait()
        OS[...] = table_right(RI[t].T, TI, ((1,), (0,)))

        def depth_half(half, put):
            for hl in range(HC):
                tw = WI[q, half * HC + hl]
                for p in range(2):
                    total = None
                    for r in range(R):
                        for c in range(2):
                            k = 2 * r + c
                            term = tw[k : k + 1] * OS[r * B : (r + 1) * B, (2 * p + c) * A : (2 * p + c + 1) * A]
                            total = term if total is None else total + term
                    put[p * B : (p + 1) * B, hl * A : (hl + 1) * A] = total

        depth_half(1 - q, PS.at[t])
        part = remote(PS.at[t], PR.at[t], psend.at[0, t], precv.at[0, t], (g, j, 1 - q))
        part.start()
        depth_half(q, RL)
        part.wait()

        CH = 16 if RW % 16 == 0 else 8

        def friction_chunk(i, c):
            chunk = pl.ds(pl.multiple_of(i * CH, CH), CH)
            guess = SG[chunk, :]
            loading = szero[chunk, :] + (RL[chunk, :] + PR[t, chunk, :]) + guess
            a = direct[chunk, :]
            ls = out_l[chunk, :]
            factor = jnp.exp(ls)
            af = a * factor
            v = guess
            for _ in range(NEWTON):
                s = v * factor
                root = jnp.sqrt(1.0 + s * s)
                size = jnp.log(jnp.abs(s) + root)
                misfit = a * jnp.where(s < 0.0, -size, size) + v - loading
                v = v - misfit / (af / root + 1.0)
            SL[t, q, chunk, :] = v
            TR[chunk, :] = side * (loading - v)
            out_l[chunk, :] = 0.75 * ls - 0.2 * jnp.log(1.0 + v * v) + 0.1
            return c

        lax.fori_loop(0, RW // CH, friction_chunk, 0)
        slip = remote(SL.at[t, q], SL.at[t, q], lsend.at[t], lrecv.at[t], (g, j, 1 - q))
        slip.start()

        def depth_terms(half, p, acc):
            for hl in range(HC):
                tw = WF[2 * g + q, half * HC + hl]
                cells = SL[t, half, p * B : (p + 1) * B, hl * A : (hl + 1) * A]
                terms = [tw[k : k + 1] * cells for k in range(2 * R)]
                acc = terms if acc is None else [x + y for x, y in zip(acc, terms)]
            return acc

        def put_terms(p, acc, add):
            for r in range(R):
                for c in range(2):
                    at = (slice(r * B, (r + 1) * B), slice((2 * p + c) * A, (2 * p + c + 1) * A))
                    US[at] = US[at] + acc[2 * r + c] if add else acc[2 * r + c]

        for p in range(2):
            put_terms(p, depth_terms(q, p, None), False)
        pltpu.make_async_copy(SL.at[t, 1 - q], SL.at[t, 1 - q], lrecv.at[t]).wait()
        for p in range(2):
            put_terms(p, depth_terms(1 - q, p, None), True)
        SF[t] = table_left(TF, US[...], ((1,), (1,)))
        here = pl.ds(j * 4, 4)

        def send_slip(step, c):
            peer = target(step)

            @pl.when(step != own_step)
            def _():
                remote(SF.at[t, pl.ds(peer * 4, 4)], RF.at[t, here], fsend.at[t], frecv.at[t], (g, peer, q)).start()

            return c

        lax.fori_loop(0, nx, send_slip, 0)
        pltpu.make_async_copy(SF.at[t, here], RF.at[t, here], frecv.at[t]).start()

        pull = TR[...]
        out_f[1, 0] = pull
        VP[0, rows_in, cols_in] = VP[0, rows_in, cols_in] - buoy[0] * (C1 * pull)
        VP[1, rows_in, cols_in] = VP[1, rows_in, cols_in] + buoy[1] * (C2 * pull)

        @pl.when(t < NSTEP - 1)
        def _():
            later = v_copies(t + 1)
            start_halo(*later[:4])
            later[4].start()

        slip.wait_send()
        pltpu.make_async_copy(RF.at[t], RF.at[t], frecv.at[t]).wait()
        x = table_right(RF[t].T, TV, ((1,), (0,)))
        xr, xi = x[:, :A], x[:, A:]
        tall = jnp.concatenate([xr * TW[0] + xi * TW[1], xi * TW[0] - xr * TW[1]], axis=0)
        fresh = table_left(L3, tall, ((1,), (0,)))
        out_s[t] = fresh
        for d in range(NSTEP - 1):
            for c in range(2):
                at = pl.ds(c * RB, RB)
                ACC[t + 1 + d, at] = ACC[t + 1 + d, at] + wts[d] * fresh[c * RB : (c + 1) * RB]
        return carry

    lax.fori_loop(0, NSTEP, step_body, 0)

    out_f[0] = VP[:, rows_in, cols_in]
    out_f[2] = SP[:, rows_in, :]
    out_f[3] = DP[:, :, cols_in]
    for t in range(NSTEP):
        count = (2 * nx - 1 if both else nx - 1) * 4
        left = RI.at[t, pl.ds(0, count)]
        pltpu.make_async_copy(left, left, isend.at[t]).wait()
        left = RF.at[t, pl.ds(0, (nx - 1) * 4)]
        pltpu.make_async_copy(left, left, fsend.at[t]).wait()


def per_device(nx, both, fields, buoyancy, stiffness, stress_zero, direct_effect, log_state, kernel, history, truncation):
    planes, rows, cols = fields.shape[2:]
    hist, modes, _, strike = history.shape
    A = 2 * nx
    B = rows // 2
    RB = modes * B
    depth = 2 * cols
    scale = 1.0 / math.sqrt(strike * depth)
    mats, vecs = make_tables(nx, rows, modes, scale)
    lag_number = lax.broadcasted_iota(jnp.int32, kernel.shape, 0)
    weights = jnp.where(lag_number < truncation[None], kernel, jnp.zeros_like(kernel))
    start = jnp.stack([
        jnp.sum(weights[t:, :, None, :] * history[: hist - t], axis=0) for t in range(NSTEP)
    ])
    start = jnp.transpose(start, (0, 2, 1, 3)).reshape(NSTEP, 2 * RB, A)
    wts = weights[: NSTEP - 1].reshape(NSTEP - 1, RB, A)
    LW = min(128, cols)
    vm = pltpu.VMEM
    dma = pltpu.SemaphoreType.DMA
    scratch = [
        vm((planes, rows + 16, cols + 2 * LW), F32),
        vm((planes, rows + 16, cols), F32),
        vm((planes, rows, cols + 2 * LW), F32),
        vm((2 * NSTEP - 1, 2 * RB, A), F32),
        vm((NSTEP, 4 * nx, RB), F32),
        vm((NSTEP, 8 * nx, RB), F32),
        vm((RB, 4 * A), F32),
        vm((NSTEP, rows, cols), F32),
        vm((rows, cols), F32),
        vm((NSTEP, rows, cols), F32),
        vm((NSTEP, 2, rows, cols), F32),
        vm((RB, 4 * A), F32),
        vm((NSTEP, 4 * nx, RB), F32),
        vm((NSTEP, 4 * nx, RB), F32),
        vm((rows, cols), F32),
        vm((rows, cols), F32),
        vm((NSTEP, 2, planes, 8, cols), F32),
        vm((NSTEP, planes, rows, LW), F32),
        vm((NSTEP, rows, cols), F32),
        vm((NSTEP, 2, planes, 8, cols), F32),
        vm((NSTEP, planes, rows, LW), F32),
        dma((NSTEP,)), dma((NSTEP,)), dma((NSTEP,)), dma((NSTEP,)),
        dma((2, NSTEP)), dma((2, NSTEP)), dma((NSTEP,)), dma((NSTEP,)),
        dma((3,)), dma((3, NSTEP)), dma((3,)), dma((3, NSTEP)), dma, dma((NSTEP,)),
    ]
    whole = pl.BlockSpec(memory_space=pltpu.VMEM)
    args = [
        fields.reshape(4, planes, rows, cols), buoyancy[0], stiffness[0], stress_zero, direct_effect, log_state,
        start, wts, *[jnp.asarray(x) for x in mats], *[jnp.asarray(x) for x in vecs],
    ]
    out_f, out_l, out_s = pl.pallas_call(
        functools.partial(kernel_body, nx, both),
        out_shape=(
            jax.ShapeDtypeStruct((4, planes, rows, cols), F32),
            jax.ShapeDtypeStruct((rows, cols), F32),
            jax.ShapeDtypeStruct((NSTEP, 2 * RB, A), F32),
        ),
        in_specs=[whole] * len(args),
        out_specs=(whole, whole, whole),
        scratch_shapes=scratch,
        compiler_params=pltpu.CompilerParams(
            collective_id=0, has_side_effects=True, vmem_limit_bytes=60 * 1024 * 1024
        ),
    )(*args)
    spectra = out_s.reshape(NSTEP, 2, modes, strike).transpose(0, 2, 1, 3)
    return out_f.reshape(4, 1, planes, rows, cols), out_l, spectra


def solution(mesh, both=True):
    return jax.shard_map(
        functools.partial(per_device, mesh.shape["gx"], both),
        mesh=mesh,
        in_specs=(
            P(None, "grp", None, "gx", "gz"),
            P("grp", None, "gx", "gz"),
            P("grp", None, "gx", "gz"),
            P("gx", "gz"),
            P("gx", "gz"),
            P("gx", "gz"),
            P(None, ("grp", "gx", "gz"), None),
            P(None, ("grp", "gx", "gz"), None, None),
            P(("grp", "gx", "gz"), None),
        ),
        out_specs=(
            P(None, "grp", None, "gx", "gz"),
            P("gx", "gz"),
            P(None, ("grp", "gx", "gz"), None, None),
        ),
        check_vma=False,
    )
```

time: 815 us -> 143 us (0.18); the launches traced: 804 us -> 143 us
  waiting for transfers between devices: 205 us -> 0 us
  starting transfers between devices: 197 us -> 0 us
  local copies, waits for them, and re-layouts: 159 us -> 7.3 us
  Pallas kernels: 0 us -> 129 us
  matrix products: 123 us -> 0 us
  other arithmetic: 104 us -> 6.59 us
  between operations: 16.4 us -> 0.73 us
    pallas_call x0 -> x1, Pallas kernels: none -> 129 us  [per_device(): pl.pallas_call(functools.partial(kernel_body, nx, both), out_shape=(jax.S...]
    psum x4 -> x0, waiting for transfers between devices: 125 us -> none  [per_device(): relief = lax.psum(own_depth, 'grp') * scale_back]
    dot_general x80 -> x0, matrix products: 123 us -> none  [the longest x4 21.5 us: per_device(): jnp.einsum('jy,jz->yz', by_rows[:, 1], back_sin, precision=FULL_PRECISION)]
    ppermute x36 -> x0, starting transfers between devices: 101 us -> none  [the longest x16 50.3 us: extended(): lax.ppermute(head, axis, [((i + 1) % count, i) for i in range(ends)])]
    all_to_all x8 -> x0, starting transfers between devices: 95 us -> none  [the longest x4 59.3 us: per_device(): lax.all_to_all(by_modes, 'gx', split_axis=0, concat_axis=2, tiled=True)]
    unnamed x116 -> x8, local copies, waits for them, and re-layouts: 73.8 us -> 2.23 us
    all_to_all x8 -> x0, waiting for transfers between devices: 43.7 us -> none  [the longest x4 27.6 us: per_device(): lax.all_to_all(by_modes, 'gx', split_axis=0, concat_axis=2, tiled=True)]
    another operation x36 -> x0, local copies, waits for them, and re-layouts: 35.3 us -> none  [the longest x12 22.5 us: strike_inverse(): jnp.stack([real_part.reshape(planes_count, total_count), imag_part.reshap...]
  transfers between devices with their start and end apart: 56 -> 0, of which waited for: 22 -> 0; matrix products, arithmetic and copies ran while one was open for 28% -> 0% of each run, Pallas kernels for 0% -> 0%
where the time goes in v1:
time: 143 us
  Pallas kernels  129 us (90%)
  local copies, waits for them, and re-layouts  7.3 us (5%)
  other arithmetic  6.59 us (5%)
    pallas_call x1, Pallas kernels, per_device(): pl.pallas_call(functools.partial(kernel_body, nx, both), out_shape=(jax.S...  129 us
    reduce_sum x4, other arithmetic, per_device(): jnp.sum(weights[t:, :, None, :] * history[:hist - t], axis=0)  4.67 us

profile of v1, /device:TPU:1, one launch (start us, length us, event | category | flops | bytes accessed | tf_op | source)
XLA Modules:
  0.0 143.2 jit_solution(16023417347852525775)
XLA Ops:
  0.6 0.0 copy-start
  0.6 1.7 %fusion = f32[16,4,4096]{2,1,0:T(4,128)S(1)} fusion(f32[16,4,4096]{2,1,0:T(4,128)} %param.24, s32[4,4096]{1,0:T(4,128)} %param.26), kind=kLoop, calls=%fused_computation.5 | loop fusion | flops 524288 | bytes 2162688 | tf_op jit(solution)/shard_map/jit(_where)/select_n | solution.py:462
  2.3 0.3 copy-done
  2.6 1.2 multiply_reduce_fusion
  3.7 0.8 reshape.28.wts
  4.6 0.1 slice.30
  4.6 1.0 multiply_reduce_fusion.3
  5.6 0.1 slice.29
  5.7 1.1 multiply_reduce_fusion.2
  6.8 0.1 slice.28
  6.9 1.4 multiply_reduce_fusion.1
  8.3 0.3 maximum_bitcast_fusion
  8.5 0.3 copy.23
  8.9 1.2 reshape.27.start
  10.1 128.6 %shard_map.193 = (f32[4,4,64,512]{3,2,1,0:T(8,128)}, f32[64,512]{1,0:T(8,128)}, f32[4,256,128]{2,1,0:T(8,128)}) custom-call(f32[4,4,64,512]{3,2,1,0:T(8,128)} %bitcast.15, f32[4,64,512]{2,1,0:T(8,128)} %bitcast.17, f32[4,64,512]{2,1,0:T(8,128)} %bitcast.18, f32[64,512]{1,0:T(8,128)} %szero.1, f32[64,512]{1,0:T(8,128)} %direct.1, f32[64,512]{1,0:T(8,128)} %logs.1, ...), custom_call_target="tpu_custom_call" | custom-call | tf_op jit(solution)/shard_map/pallas_call | solution.py:502
  138.7 0.0 copy-start.1
  138.7 1.4 reshape.30
  140.0 1.2 copy.27
  141.2 0.0 copy-done.1
  141.2 0.0 copy-start.2
  141.2 1.3 copy.30
  142.6 0.0 copy-done.2
  142.6 0.7 copy.31
  (1 shorter events, 0.0 us)
Async XLA Ops:
  0.6 1.9 %copy-start = (f32[16,4,2,4096]{3,2,1,0:T(2,128)S(1)}, f32[16,4,2,4096]{3,2,1,0:T(2,128)}, u32[]{:S(2)}) copy-start(f32[16,4,2,4096]{3,2,1,0:T(2,128)} %param.25) | copy-start | bytes 6291460
  138.7 2.6 %copy-start.1 = (f32[4,4,64,512]{3,2,1,0:T(8,128)S(1)}, f32[4,4,64,512]{3,2,1,0:T(8,128)}, u32[]{:S(2)}) copy-start(f32[4,4,64,512]{3,2,1,0:T(8,128)} %get-tuple-element.6) | copy-start | bytes 6291460
  141.2 1.3 copy-start.2

commit v2 on v1

v2 whole, which is shorter than its diff:
```python
import functools
import math

import jax
import jax.numpy as jnp
import numpy as np
from jax import lax
from jax.experimental import pallas as pl
from jax.experimental.pallas import tpu as pltpu
from jax.sharding import PartitionSpec as P

NSTEP = 4
NEWTON = 4
C1 = 9.0 / 8.0
C2 = 1.0 / 24.0
MESH = pl.DeviceIdType.MESH
BF = jnp.bfloat16
F32 = jnp.float32


def split_table(table):
    hi = np.asarray(table, np.float32).astype(jnp.bfloat16)
    lo = (table - hi.astype(np.float64)).astype(jnp.bfloat16)
    return np.stack([hi, lo])


def cis(turns):
    return np.cos(2 * np.pi * turns), np.sin(2 * np.pi * turns)


def make_tables(nx, rows, modes, scale):
    A = 2 * nx
    B = rows // 2
    R = modes
    depth = 4 * nx * R
    strike = nx * rows
    eye_r = np.eye(R)
    eye_p = np.eye(2)
    m, b, k, a = np.arange(B), np.arange(B), np.arange(A), np.arange(A)
    c, s = cis(np.outer(m, b) / B)
    inv = np.array([[c, -s], [s, c]])
    fwd = np.array([[c, s], [-s, c]])
    L1 = np.einsum("xybm,rs->xrbsmy", inv, eye_r).reshape(2 * R * B, 2 * R * B)
    L3 = np.einsum("xymb,rs->rmxysb", fwd, eye_r).reshape(2 * R * B, 2 * R * B) * scale
    c, s = cis(np.outer(b, k) / strike)
    twiddle = np.stack([np.tile(c, (R, 1)), np.tile(s, (R, 1))])
    c, s = cis(np.outer(a, k) / A)
    inv = np.array([[c, -s], [s, c]]).reshape(2, 2, nx, 2, A)
    T2 = np.einsum("xyjpk->jxpyk", inv).reshape(4 * nx, 2 * A)
    fwd = np.array([[c, s], [-s, c]]).reshape(2, 2, nx, 2, A)
    TV = np.einsum("xyjpk->jpyxk", fwd).reshape(4 * nx, 2 * A)
    i, z = np.arange(nx), np.arange(A)
    c, s = cis(np.outer(i, z) / A)
    sign = np.where(np.arange(2)[:, None] * z[None, :] % 2 == 1, -1.0, 1.0)
    inv = np.array([[c, -s], [s, c]])
    TI = np.einsum("xyiz,gz,pn->giypnxz", inv, sign, eye_p).reshape(8 * nx, 4 * A)
    fwd = np.array([[c, s], [-s, c]])
    TF = np.einsum("xyiz,pn->ipxnyz", fwd, eye_p).reshape(4 * nx, 4 * A)
    zz = np.arange(depth).reshape(2 * R, 1, A)
    r = np.arange(R)[None, :, None]
    wi, wf = [], []
    for q in range(2):
        c, s = cis((R * q + r) * zz / depth)
        wi.append(np.stack([c, -s], axis=2).reshape(2 * R, 2 * R, A) * scale)
    for g in range(2):
        for q in range(2):
            c, s = cis((R * q + r) * zz / depth)
            wf.append(np.stack([c, -s], axis=2).reshape(2 * R, 2 * R, A) * sign[g])
    mats = [split_table(x) for x in (L1, T2, TI, TF, TV, L3)]
    return mats, [np.asarray(x, np.float32) for x in (twiddle, np.stack(wi), np.stack(wf))]


def split(x):
    hi = x.astype(BF)
    return hi, (x - hi.astype(F32)).astype(BF)


def dot(x, y, dims):
    return lax.dot_general(x, y, (dims, ((), ())), preferred_element_type=F32)


def table_left(tab, x, dims):
    hi, lo = split(x)
    return dot(tab[0], hi, dims) + (dot(tab[0], lo, dims) + dot(tab[1], hi, dims))


def table_right(x, tab, dims):
    hi, lo = split(x)
    return dot(hi, tab[0], dims) + (dot(lo, tab[0], dims) + dot(hi, tab[1], dims))


def roll(x, shift, axis):
    return pltpu.roll(x, shift % x.shape[axis], axis)


def kernel_body(
    nx, fields_h, buoy_h, stiff_h, szero_h, direct_h, logs_h, kern_h, hist_h, trunc_h,
    L1_h, T2_h, TI_h, TF_h, TV_h, L3_h, TW_h, WI_h, WF_h,
    out_f, out_l, out_s,
    buoy, stiff, szero, direct, LS, KW, H, TRN, L1, T2, TI, TF, TV, L3, TW, WI, WF, WD, NS, FR,
    VP, SP, DP, ACC, GS, RI, OS, PS, RL, PR, SL, US, SF, RF, TR, SG, HV, DV, NP, HS, DS,
    insem, outsem, isend, irecv, fsend, frecv, psend, precv, lsend, lrecv, vsend, vrecv, ssend, srecv, gsend, grecv,
):
    g, j, q = lax.axis_index("grp"), lax.axis_index("gx"), lax.axis_index("gz")
    A = 2 * nx
    RB = TW.shape[1]
    RW, CW = szero.shape
    B = RW // 2
    R = RB // B
    LW = DV.shape[3]
    HC = CW // A
    HIST = H.shape[0]
    side = (2 * g - 1).astype(F32)
    rows_in = pl.ds(8, RW)
    cols_in = pl.ds(LW, CW)

    if nx == 64:
        turn = (2, 3, 1, 0)
        xs = [lax.rem(lax.div(j, 16) + k, 4) * 16 for k in turn]
        ys = [lax.rem(j, 4) + k for k in turn]
        peers_xy = [x + lax.rem(y, 4) for x in xs for y in ys]
        zs = lax.rem(lax.div(j, 4), 4)
        outer = 4

        def layer(i):
            return lax.rem(zs + i + 2, 4) * 4

        own_layer, own_xy = 2, 15
    else:
        peers_xy = [j * 0]
        outer = nx

        def layer(i):
            return lax.rem(j + i + 1, nx)

        own_layer, own_xy = nx - 1, 0

    def each_peer(act):
        def one_layer(i, carry):
            z = layer(i)
            for n, xy in enumerate(peers_xy):
                if n == own_xy:

                    @pl.when(i != own_layer)
                    def _():
                        act(z + xy)
                else:
                    act(z + xy)
            return carry

        lax.fori_loop(0, outer, one_layer, 0)

    barrier = pltpu.get_barrier_semaphore()

    def greet(peer):
        pl.semaphore_signal(barrier, inc=1, device_id=(g, peer, q), device_id_type=MESH)
        pl.semaphore_signal(barrier, inc=1, device_id=(1 - g, peer, q), device_id_type=MESH)

    each_peer(greet)
    pl.semaphore_signal(barrier, inc=1, device_id=(1 - g, j, q), device_id_type=MESH)
    pl.semaphore_signal(barrier, inc=1, device_id=(g, j, 1 - q), device_id_type=MESH)

    pairs = [
        (kern_h, KW), (trunc_h, TRN), (hist_h, H), (L1_h, L1), (TW_h, TW), (T2_h, T2),
        (fields_h.at[0], VP.at[:, rows_in, cols_in]), (stiff_h, stiff), (fields_h.at[2], SP.at[:, rows_in, :]),
        (fields_h.at[3], DP.at[:, :, cols_in]), (fields_h.at[1], NS), (TI_h, TI), (WI_h, WI), (szero_h, szero),
        (direct_h, direct), (logs_h, LS), (WF_h, WF), (TF_h, TF), (buoy_h, buoy), (TV_h, TV), (L3_h, L3),
    ]
    loads = [pltpu.make_async_copy(src, dst, insem.at[n]) for n, (src, dst) in enumerate(pairs)]
    for copy in loads:
        copy.start()
    for t in range(ACC.shape[0]):
        ACC[t] = jnp.zeros((2 * RB, A), F32)
    VP[:, pl.ds(0, 8), :] = jnp.zeros((4, 8, CW + 2 * LW), F32)
    VP[:, pl.ds(8 + RW, 8), :] = jnp.zeros((4, 8, CW + 2 * LW), F32)
    VP[:, rows_in, pl.ds(0, LW)] = jnp.zeros((4, RW, LW), F32)
    VP[:, rows_in, pl.ds(LW + CW, LW)] = jnp.zeros((4, RW, LW), F32)
    SP[:, pl.ds(0, 8), :] = jnp.zeros((4, 8, CW), F32)
    SP[:, pl.ds(8 + RW, 8), :] = jnp.zeros((4, 8, CW), F32)
    DP[:, :, pl.ds(0, LW)] = jnp.zeros((4, RW, LW), F32)
    DP[:, :, pl.ds(LW + CW, LW)] = jnp.zeros((4, RW, LW), F32)

    loads[0].wait()
    loads[1].wait()

    def mask_lag(lag, carry):
        for r in range(R):
            pick = pl.ds(r, B, stride=R)
            kept = jnp.where(lag < TRN[pick, :], KW[lag, pick, :], 0.0)
            for c in range(2):
                WD[lag, pl.ds(r * 2 * B + c, B, stride=2), :] = kept
        return carry

    lax.fori_loop(0, HIST, mask_lag, 0)

    def lag_sums(ahead):
        for r in range(R):
            part = pl.ds(r * 2 * B, 2 * B)

            def one_lag(lag, total):
                return total + WD[lag + ahead, part, :] * H[lag, part, :]

            ACC[ahead, part, :] = lax.fori_loop(0, HIST - ahead, one_lag, ACC[ahead, part, :])

    for copy in loads[2:6]:
        copy.wait()
    lag_sums(0)
    loads[6].wait()
    pl.semaphore_wait(barrier, 2 * (nx - 1) + 2)

    def remote(src, dst, send, recv, device):
        return pltpu.make_async_remote_copy(
            src_ref=src, dst_ref=dst, send_sem=send, recv_sem=recv, device_id=device, device_id_type=MESH
        )

    def row_copies(src_of, land, t, send, recv):
        up = remote(src_of(pl.ds(RW, 8)), land.at[t, 0], send.at[0], recv.at[0, t], (g, lax.rem(j + 1, nx), q))
        down = remote(src_of(pl.ds(8, 8)), land.at[t, 1], send.at[1], recv.at[1, t], (g, lax.rem(j + nx - 1, nx), q))
        return up, down

    def v_copies(t):
        up, down = row_copies(lambda d: VP.at[:, d, cols_in], HV, t, vsend, vrecv)
        right = remote(VP.at[:, rows_in, pl.ds(CW, LW)], DV.at[t], vsend.at[2], vrecv.at[2, t], (g, j, 1 - q))
        left = remote(VP.at[:, rows_in, pl.ds(LW, LW)], DV.at[t], vsend.at[2], vrecv.at[2, t], (g, j, 1 - q))
        across = remote(VP.at[0, rows_in, cols_in], NP.at[t], gsend, grecv.at[t], (1 - g, j, q))
        return up, down, right, left, across

    def s_copies(t):
        up, down = row_copies(lambda d: SP.at[:, d, :], HS, t, ssend, srecv)
        right = remote(DP.at[:, :, pl.ds(CW, LW)], DS.at[t], ssend.at[2], srecv.at[2, t], (g, j, 1 - q))
        left = remote(DP.at[:, :, pl.ds(LW, LW)], DS.at[t], ssend.at[2], srecv.at[2, t], (g, j, 1 - q))
        return up, down, right, left

    def start_halo(up, down, right, left):
        @pl.when(j < nx - 1)
        def _():
            up.start()

        @pl.when(j > 0)
        def _():
            down.start()

        @pl.when(q == 0)
        def _():
            right.start()

        @pl.when(q == 1)
        def _():
            left.start()

    def sent_halo(up, down, right, left):
        @pl.when(j < nx - 1)
        def _():
            up.wait_send()

        @pl.when(j > 0)
        def _():
            down.wait_send()

        right.wait_send()

    def recv_halo(up, down, right, t, land, depth_land, put_rows, put_cols):
        @pl.when(j > 0)
        def _():
            up.wait_recv()
            put_rows(0, land[t, 0])

        @pl.when(j < nx - 1)
        def _():
            down.wait_recv()
            put_rows(8 + RW, land[t, 1])

        right.wait_recv()

        @pl.when(q == 0)
        def _():
            put_cols(LW + CW, depth_land[t])

        @pl.when(q == 1)
        def _():
            put_cols(0, depth_land[t])

    def v_rows(at, x):
        VP[:, pl.ds(at, 8), cols_in] = x

    def v_cols(at, x):
        VP[:, rows_in, pl.ds(at, LW)] = x

    def s_rows(at, x):
        SP[:, pl.ds(at, 8), :] = x

    def d_cols(at, x):
        DP[:, :, pl.ds(at, LW)] = x

    first = v_copies(0)
    start_halo(*first[:4])
    first[4].start()

    def out_copies():
        return [
            pltpu.make_async_copy(SP.at[:, rows_in, :], out_f.at[2], outsem.at[0]),
            pltpu.make_async_copy(DP.at[:, :, cols_in], out_f.at[3], outsem.at[1]),
            pltpu.make_async_copy(VP.at[:, rows_in, cols_in], out_f.at[0], outsem.at[2]),
            pltpu.make_async_copy(NS, out_f.at[1], outsem.at[3]),
            pltpu.make_async_copy(LS, out_l, outsem.at[4]),
        ]

    def step_body(t, carry):
        x = table_left(L1, ACC[t], ((1,), (0,)))
        xr, xi = x[:RB], x[RB:]
        wide = jnp.concatenate([xr * TW[0] - xi * TW[1], xr * TW[1] + xi * TW[0]], axis=1)
        GS[t] = table_left(T2, wide, ((1,), (1,)))
        mine = pl.ds((g * nx + j) * 4, 4)

        def send_modes(peer):
            block = GS.at[t, pl.ds(peer * 4, 4)]
            remote(block, RI.at[t, mine], isend.at[t], irecv.at[t], (1 - g, peer, q)).start()
            remote(block, RI.at[t, mine], isend.at[t], irecv.at[t], (g, peer, q)).start()

        each_peer(send_modes)
        own = GS.at[t, pl.ds(j * 4, 4)]
        remote(own, RI.at[t, mine], isend.at[t], irecv.at[t], (1 - g, j, q)).start()
        pltpu.make_async_copy(own, RI.at[t, mine], irecv.at[t]).start()

        @pl.when(t == 0)
        def _():
            for copy in loads[7:11]:
                copy.wait()

        up, down, right, left, across = v_copies(t)
        recv_halo(up, down, right, t, HV, DV, v_rows, v_cols)
        sent_halo(up, down, right, left)

        def stress_chunk(i, c):
            r0 = pl.multiple_of(i * 8, 8)
            chunk = pl.ds(r0, 8)
            inner = pl.ds(r0 + 8, 8)
            vs = []
            for p in range(4):
                tall = VP[p, pl.ds(r0, 24), cols_in]
                wide = VP[p, inner, :]
                v = tall[8:16]
                vs.append(v)
                st = stiff[p, chunk, :]
                up1, up2, dn1 = (roll(tall, s, 0)[8:16] for s in (-1, -2, 1))
                SP[p, inner, :] = SP[p, inner, :] + st * (C1 * (up1 - v) - C2 * (up2 - dn1))
                up1, up2, dn1 = (roll(wide, s, 1)[:, LW : LW + CW] for s in (-1, -2, 1))
                DP[p, chunk, cols_in] = DP[p, chunk, cols_in] + st * (C1 * (up1 - v) - C2 * (up2 - dn1))
            for p in range(1, 4):
                far = 0.0 - (vs[p - 2] if p >= 2 else 0.0)
                if p < 3:
                    far = vs[p + 1] + far
                NS[p, chunk, :] = NS[p, chunk, :] + stiff[p, chunk, :] * (C1 * (vs[p] - vs[p - 1]) - C2 * far)
            return c

        lax.fori_loop(0, RW // 8, stress_chunk, 0)
        up, down, right, left = s_copies(t)
        start_halo(up, down, right, left)

        @pl.when(t == NSTEP - 1)
        def _():
            for copy in out_copies()[:2]:
                copy.start()

        across.wait()
        SG[...] = side * (VP[0, rows_in, cols_in] - NP[t])

        @pl.when(t < NSTEP - 1)
        def _():
            lag_sums(t + 1)

        @pl.when(t == 0)
        def _():
            for copy in loads[11:]:
                copy.wait()

        pltpu.make_async_copy(RI.at[t], RI.at[t], irecv.at[t]).wait()
        OS[...] = table_right(RI[t].T, TI, ((1,), (0,)))

        def depth_half(half, p, put):
            for hl in range(HC):
                tw = WI[q, half * HC + hl]
                total = None
                for k in range(2 * R):
                    r, c = k // 2, k % 2
                    term = tw[k : k + 1] * OS[r * B : (r + 1) * B, (2 * p + c) * A : (2 * p + c + 1) * A]
                    total = term if total is None else total + term
                put[p * B : (p + 1) * B, hl * A : (hl + 1) * A] = total

        parts = []
        for p in range(2):
            depth_half(1 - q, p, PS.at[t])
            here = pl.ds(p * B, B)
            part = remote(PS.at[t, here], PR.at[t, here], psend.at[p, t], precv.at[p, t], (g, j, 1 - q))
            part.start()
            parts.append(part)
        for p in range(2):
            depth_half(q, p, RL)

        CH = 16

        def friction_chunk(i, c):
            chunk = pl.ds(pl.multiple_of(i * CH, CH), CH)
            guess = SG[chunk, :]
            loading = szero[chunk, :] + (RL[chunk, :] + PR[t, chunk, :]) + guess
            a = direct[chunk, :]
            ls = LS[chunk, :]
            factor = jnp.exp(ls)
            af = a * factor
            v = guess
            for _ in range(NEWTON):
                s = v * factor
                root = jnp.sqrt(1.0 + s * s)
                size = jnp.log(jnp.abs(s) + root)
                misfit = a * jnp.where(s < 0.0, -size, size) + v - loading
                v = v - misfit / (af / root + 1.0)
            SL[t, q, chunk, :] = v
            TR[chunk, :] = side * (loading - v)
            LS[chunk, :] = 0.75 * ls - 0.2 * jnp.log(1.0 + v * v) + 0.1
            return c

        slips = []
        for p in range(2):
            parts[p].wait_recv()
            lax.fori_loop(p * B // CH, (p + 1) * B // CH, friction_chunk, 0)
            here = pl.ds(p * B, B)
            slip = remote(SL.at[t, q, here], SL.at[t, q, here], lsend.at[p, t], lrecv.at[p, t], (g, j, 1 - q))
            slip.start()
            slips.append(slip)

        def depth_terms(half, p, add):
            acc = None
            for hl in range(HC):
                tw = WF[2 * g + q, half * HC + hl]
                cells = SL[t, half, p * B : (p + 1) * B, hl * A : (hl + 1) * A]
                terms = [tw[k : k + 1] * cells for k in range(2 * R)]
                acc = terms if acc is None else [x + y for x, y in zip(acc, terms)]
            for k in range(2 * R):
                r, c = k // 2, k % 2
                at = (slice(r * B, (r + 1) * B), slice((2 * p + c) * A, (2 * p + c + 1) * A))
                US[at] = US[at] + acc[k] if add else acc[k]

        for p in range(2):
            depth_terms(q, p, False)
        for p in range(2):
            here = pl.ds(p * B, B)
            land = SL.at[t, 1 - q, here]
            pltpu.make_async_copy(land, land, lrecv.at[p, t]).wait()
            depth_terms(1 - q, p, True)
        SF[t] = table_left(TF, US[...], ((1,), (1,)))
        spot = pl.ds(j * 4, 4)

        def send_slip(peer):
            remote(SF.at[t, pl.ds(peer * 4, 4)], RF.at[t, spot], fsend.at[t], frecv.at[t], (g, peer, q)).start()

        each_peer(send_slip)
        pltpu.make_async_copy(SF.at[t, spot], RF.at[t, spot], frecv.at[t]).start()

        recv_halo(up, down, right, t, HS, DS, s_rows, d_cols)
        sent_halo(up, down, right, left)
        NS[0] = TR[...]

        def velocity_chunk(i, c):
            r0 = pl.multiple_of(i * 8, 8)
            chunk = pl.ds(r0, 8)
            inner = pl.ds(r0 + 8, 8)
            n0, n1, n2, n3 = (NS[p, chunk, :] for p in range(4))
            plane_terms = [
                C1 * (n1 - n0) - C2 * n2,
                C1 * (n2 - n1) - C2 * (n3 - n0),
                C1 * (n3 - n2) + C2 * n1,
                C2 * n2 - C1 * n3,
            ]
            for p in range(4):
                tall = SP[p, pl.ds(r0, 24), :]
                wide = DP[p, chunk, :]
                dn1, dn2, up1 = (roll(tall, s, 0)[8:16] for s in (1, 2, -1))
                total = plane_terms[p] + (C1 * (tall[8:16] - dn1) - C2 * (up1 - dn2))
                dn1, dn2, up1 = (roll(wide, s, 1)[:, LW : LW + CW] for s in (1, 2, -1))
                total = total + (C1 * (wide[:, LW : LW + CW] - dn1) - C2 * (up1 - dn2))
                VP[p, inner, cols_in] = VP[p, inner, cols_in] + buoy[p, chunk, :] * total
            return c

        lax.fori_loop(0, RW // 8, velocity_chunk, 0)

        @pl.when(t < NSTEP - 1)
        def _():
            later = v_copies(t + 1)
            start_halo(*later[:4])
            later[4].start()

        @pl.when(t == NSTEP - 1)
        def _():
            for copy in out_copies()[2:]:
                copy.start()

        for p in range(2):
            parts[p].wait_send()
            slips[p].wait_send()
        pltpu.make_async_copy(RF.at[t], RF.at[t], frecv.at[t]).wait()
        x = table_right(RF[t].T, TV, ((1,), (0,)))
        xr, xi = x[:, :A], x[:, A:]
        tall = jnp.concatenate([xr * TW[0] + xi * TW[1], xi * TW[0] - xr * TW[1]], axis=0)
        fresh = table_left(L3, tall, ((1,), (0,)))
        FR[t] = fresh
        for d in range(NSTEP - 1):
            ACC[t + 1 + d] = ACC[t + 1 + d] + WD[d] * fresh
        pltpu.make_async_copy(FR.at[t], out_s.at[t], outsem.at[5 + t]).start()
        return carry

    lax.fori_loop(0, NSTEP, step_body, 0)

    for copy in out_copies():
        copy.wait()
    for t in range(NSTEP):
        pltpu.make_async_copy(FR.at[t], out_s.at[t], outsem.at[5 + t]).wait()
        left = RI.at[t, pl.ds(0, (2 * nx - 1) * 4)]
        pltpu.make_async_copy(left, left, isend.at[t]).wait()
        left = RF.at[t, pl.ds(0, (nx - 1) * 4)]
        pltpu.make_async_copy(left, left, fsend.at[t]).wait()


def per_device(nx, fields, buoyancy, stiffness, stress_zero, direct_effect, log_state, kernel, history, truncation):
    planes, rows, cols = fields.shape[2:]
    hist, modes, _, strike = history.shape
    A = 2 * nx
    B = rows // 2
    RB = modes * B
    depth = 2 * cols
    scale = 1.0 / math.sqrt(strike * depth)
    mats, vecs = make_tables(nx, rows, modes, scale)
    kernel = kernel.reshape(hist, modes, B, A).transpose(0, 2, 1, 3).reshape(hist, RB, A)
    history = history.reshape(hist, modes, 2, B, A).transpose(0, 1, 3, 2, 4).reshape(hist, 2 * RB, A)
    truncation = truncation.reshape(modes, B, A).transpose(1, 0, 2).reshape(RB, A)
    LW = min(128, cols)
    vm = pltpu.VMEM
    dma = pltpu.SemaphoreType.DMA
    args = [
        fields.reshape(4, planes, rows, cols), buoyancy[0], stiffness[0], stress_zero, direct_effect, log_state,
        kernel, history, truncation, *[jnp.asarray(x) for x in mats], *[jnp.asarray(x) for x in vecs],
    ]
    scratch = [vm(x.shape, x.dtype) for x in args[1:]] + [
        vm((hist, 2 * RB, A), F32),
        vm((planes, rows, cols), F32),
        vm((NSTEP, 2 * RB, A), F32),
        vm((planes, rows + 16, cols + 2 * LW), F32),
        vm((planes, rows + 16, cols), F32),
        vm((planes, rows, cols + 2 * LW), F32),
        vm((2 * NSTEP - 1, 2 * RB, A), F32),
        vm((NSTEP, 4 * nx, RB), F32),
        vm((NSTEP, 8 * nx, RB), F32),
        vm((RB, 4 * A), F32),
        vm((NSTEP, rows, cols), F32),
        vm((rows, cols), F32),
        vm((NSTEP, rows, cols), F32),
        vm((NSTEP, 2, rows, cols), F32),
        vm((RB, 4 * A), F32),
        vm((NSTEP, 4 * nx, RB), F32),
        vm((NSTEP, 4 * nx, RB), F32),
        vm((rows, cols), F32),
        vm((rows, cols), F32),
        vm((NSTEP, 2, planes, 8, cols), F32),
        vm((NSTEP, planes, rows, LW), F32),
        vm((NSTEP, rows, cols), F32),
        vm((NSTEP, 2, planes, 8, cols), F32),
        vm((NSTEP, planes, rows, LW), F32),
        dma((21,)), dma((5 + NSTEP,)),
        dma((NSTEP,)), dma((NSTEP,)), dma((NSTEP,)), dma((NSTEP,)),
        dma((2, NSTEP)), dma((2, NSTEP)), dma((2, NSTEP)), dma((2, NSTEP)),
        dma((3,)), dma((3, NSTEP)), dma((3,)), dma((3, NSTEP)), dma, dma((NSTEP,)),
    ]
    hbm = pl.BlockSpec(memory_space=pl.ANY)
    out_f, out_l, out_s = pl.pallas_call(
        functools.partial(kernel_body, nx),
        out_shape=(
            jax.ShapeDtypeStruct((4, planes, rows, cols), F32),
            jax.ShapeDtypeStruct((rows, cols), F32),
            jax.ShapeDtypeStruct((NSTEP, 2 * RB, A), F32),
        ),
        in_specs=[hbm] * len(args),
        out_specs=(hbm, hbm, hbm),
        scratch_shapes=scratch,
        compiler_params=pltpu.CompilerParams(
            collective_id=0, has_side_effects=True, vmem_limit_bytes=60 * 1024 * 1024
        ),
    )(*args)
    spectra = out_s.reshape(NSTEP, modes, B, 2, A).transpose(0, 1, 3, 2, 4).reshape(NSTEP, modes, 2, strike)
    return out_f.reshape(4, 1, planes, rows, cols), out_l, spectra


def solution(mesh):
    return jax.shard_map(
        functools.partial(per_device, mesh.shape["gx"]),
        mesh=mesh,
        in_specs=(
            P(None, "grp", None, "gx", "gz"),
            P("grp", None, "gx", "gz"),
            P("grp", None, "gx", "gz"),
            P("gx", "gz"),
            P("gx", "gz"),
            P("gx", "gz"),
            P(None, ("grp", "gx", "gz"), None),
            P(None, ("grp", "gx", "gz"), None, None),
            P(("grp", "gx", "gz"), None),
        ),
        out_specs=(
            P(None, "grp", None, "gx", "gz"),
            P("gx", "gz"),
            P(None, ("grp", "gx", "gz"), None, None),
        ),
        check_vma=False,
    )
```

time: 143 us -> 116 us (0.81)
  Pallas kernels: 129 us -> 111 us
  other arithmetic: 6.59 us -> 0 us
  local copies, waits for them, and re-layouts: 7.3 us -> 4.66 us
    pallas_call x1, Pallas kernels: 129 us -> 111 us  [per_device(): pl.pallas_call(functools.partial(kernel_body, nx), out_shape=(jax.ShapeDt...]
    reduce_sum x4 -> x0, other arithmetic: 4.67 us -> none  [per_device(): jnp.sum(weights[t:, :, None, :] * history[:hist - t], axis=0)]
    reshape x4 -> x0, local copies, waits for them, and re-layouts: 4.53 us -> none  [the longest x2 2.56 us: per_device(): spectra = out_s.reshape(NSTEP, 2, modes, strike).transpose(0, 2, 1, 3)]
    unnamed x8 -> x7, local copies, waits for them, and re-layouts: 2.23 us -> 4.66 us
    select_n x1 -> x0, other arithmetic: 1.66 us -> none  [per_device(): jnp.where(lag_number < truncation[None], kernel, jnp.zeros_like(kernel))]
where the time goes in v2:
time: 116 us
  Pallas kernels  111 us (96%)
  local copies, waits for them, and re-layouts  4.66 us (4%)
    pallas_call x1, Pallas kernels, per_device(): pl.pallas_call(functools.partial(kernel_body, nx), out_shape=(jax.ShapeDt...  111 us
    unnamed x7, local copies, waits for them, and re-layouts  4.66 us

profile of v2, /device:TPU:1, one launch (start us, length us, event | category | flops | bytes accessed | tf_op | source)
XLA Modules:
  0.0 115.8 jit_solution(4503423047367014796)
XLA Ops:
  0.6 110.5 %shard_map.193 = (f32[4,4,64,512]{3,2,1,0:T(8,128)}, f32[64,512]{1,0:T(8,128)}, f32[4,256,128]{2,1,0:T(8,128)}) custom-call(f32[4,4,64,512]{3,2,1,0:T(8,128)} %bitcast.26, f32[4,64,512]{2,1,0:T(8,128)} %bitcast.30, f32[4,64,512]{2,1,0:T(8,128)} %bitcast.31, f32[64,512]{1,0:T(8,128)} %szero_h.1, f32[64,512]{1,0:T(8,128)} %direct_h.1, f32[64,512]{1,0:T(8,128)} %logs_h.1, ...), custom_call_target="tpu_custom_call" | custom-call | tf_op jit(solution)/shard_map/pallas_call | solution.py:573
  111.2 0.0 copy-start.1
  111.2 0.0 copy-start
  111.2 3.2 %copy.29 = f32[4,1,4,64,512]{4,3,2,1,0:T(8,128)} copy(f32[4,1,4,64,512]{4,3,2,1,0:T(8,128)} %bitcast.28) | data formatting | bytes 4194304
  114.4 0.0 copy-done.1
  114.4 0.7 copy.30
  115.1 0.0 copy-done
  115.1 0.8 copy.31
Async XLA Ops:
  111.2 3.2 %copy-start.1 = (f32[64,512]{1,0:T(8,128)S(1)}, f32[64,512]{1,0:T(8,128)}, u32[]{:S(2)}) copy-start(f32[64,512]{1,0:T(8,128)} %get-tuple-element.16) | copy-start | bytes 393220
  111.2 3.9 %copy-start = (f32[4,256,128]{2,1,0:T(8,128)S(1)}, f32[4,256,128]{2,1,0:T(8,128)}, u32[]{:S(2)}) copy-start(f32[4,256,128]{2,1,0:T(8,128)} %get-tuple-element.8) | copy-start | bytes 1572868

commit v3 on v2

--- a/solution.py
+++ b/solution.py
@@ -98,7 +98,7 @@
     L1_h, T2_h, TI_h, TF_h, TV_h, L3_h, TW_h, WI_h, WF_h,
     out_f, out_l, out_s,
     buoy, stiff, szero, direct, LS, KW, H, TRN, L1, T2, TI, TF, TV, L3, TW, WI, WF, WD, NS, FR,
-    VP, SP, DP, ACC, GS, RI, OS, PS, RL, PR, SL, US, SF, RF, TR, SG, HV, DV, NP, HS, DS,
+    VP, SP, DP, ACC, GS, RI, OS, PS, RL, PR, SL, US, SF, RF, TR, SG, HV, DV, NP, HS, DS, HO,
     insem, outsem, isend, irecv, fsend, frecv, psend, precv, lsend, lrecv, vsend, vrecv, ssend, srecv, gsend, grecv,
 ):
     g, j, q = lax.axis_index("grp"), lax.axis_index("gx"), lax.axis_index("gz")
@@ -213,20 +213,25 @@
             src_ref=src, dst_ref=dst, send_sem=send, recv_sem=recv, device_id=device, device_id_type=MESH
         )
 
-    def row_copies(src_of, land, t, send, recv):
-        up = remote(src_of(pl.ds(RW, 8)), land.at[t, 0], send.at[0], recv.at[0, t], (g, lax.rem(j + 1, nx), q))
-        down = remote(src_of(pl.ds(8, 8)), land.at[t, 1], send.at[1], recv.at[1, t], (g, lax.rem(j + nx - 1, nx), q))
+    def row_copies(kind, land, t, send, recv):
+        up = remote(HO.at[kind, 0], land.at[t, 0], send.at[0], recv.at[0, t], (g, lax.rem(j + 1, nx), q))
+        down = remote(HO.at[kind, 1], land.at[t, 1], send.at[1], recv.at[1, t], (g, lax.rem(j + nx - 1, nx), q))
         return up, down
 
+    def pack_rows(kind, ref, cols):
+        for p in range(4):
+            HO[kind, 0, 2 * p : 2 * p + 2, :] = ref[p, pl.ds(RW + 6, 2), cols]
+            HO[kind, 1, 2 * p : 2 * p + 2, :] = ref[p, pl.ds(8, 2), cols]
+
     def v_copies(t):
-        up, down = row_copies(lambda d: VP.at[:, d, cols_in], HV, t, vsend, vrecv)
+        up, down = row_copies(0, HV, t, vsend, vrecv)
         right = remote(VP.at[:, rows_in, pl.ds(CW, LW)], DV.at[t], vsend.at[2], vrecv.at[2, t], (g, j, 1 - q))
         left = remote(VP.at[:, rows_in, pl.ds(LW, LW)], DV.at[t], vsend.at[2], vrecv.at[2, t], (g, j, 1 - q))
         across = remote(VP.at[0, rows_in, cols_in], NP.at[t], gsend, grecv.at[t], (1 - g, j, q))
         return up, down, right, left, across
 
     def s_copies(t):
-        up, down = row_copies(lambda d: SP.at[:, d, :], HS, t, ssend, srecv)
+        up, down = row_copies(1, HS, t, ssend, srecv)
         right = remote(DP.at[:, :, pl.ds(CW, LW)], DS.at[t], ssend.at[2], srecv.at[2, t], (g, j, 1 - q))
         left = remote(DP.at[:, :, pl.ds(LW, LW)], DS.at[t], ssend.at[2], srecv.at[2, t], (g, j, 1 - q))
         return up, down, right, left
@@ -263,7 +268,7 @@
         @pl.when(j > 0)
         def _():
             up.wait_recv()
-            put_rows(0, land[t, 0])
+            put_rows(6, land[t, 0])
 
         @pl.when(j < nx - 1)
         def _():
@@ -281,17 +286,20 @@
             put_cols(0, depth_land[t])
 
     def v_rows(at, x):
-        VP[:, pl.ds(at, 8), cols_in] = x
+        for p in range(4):
+            VP[p, pl.ds(at, 2), cols_in] = x[2 * p : 2 * p + 2]
 
     def v_cols(at, x):
         VP[:, rows_in, pl.ds(at, LW)] = x
 
     def s_rows(at, x):
-        SP[:, pl.ds(at, 8), :] = x
+        for p in range(4):
+            SP[p, pl.ds(at, 2), :] = x[2 * p : 2 * p + 2]
 
     def d_cols(at, x):
         DP[:, :, pl.ds(at, LW)] = x
 
+    pack_rows(0, VP, cols_in)
     first = v_copies(0)
     start_halo(*first[:4])
     first[4].start()
@@ -354,6 +362,7 @@
             return c
 
         lax.fori_loop(0, RW // 8, stress_chunk, 0)
+        pack_rows(1, SP, slice(None))
         up, down, right, left = s_copies(t)
         start_halo(up, down, right, left)
 
@@ -485,6 +494,7 @@
 
         @pl.when(t < NSTEP - 1)
         def _():
+            pack_rows(0, VP, cols_in)
             later = v_copies(t + 1)
             start_halo(*later[:4])
             later[4].start()
@@ -518,6 +528,18 @@
         pltpu.make_async_copy(left, left, isend.at[t]).wait()
         left = RF.at[t, pl.ds(0, (nx - 1) * 4)]
         pltpu.make_async_copy(left, left, fsend.at[t]).wait()
+
+
+def hand_over(f_in, l_in, s_in, f_out, l_out, s_out, f, l, s, sem):
+    pieces = [(f_in.at[n], f.at[n], f_out.at[n]) for n in range(f.shape[0])]
+    pieces += [(s_in, s, s_out), (l_in, l, l_out)]
+    for n, (src, mid, _) in enumerate(pieces):
+        pltpu.make_async_copy(src, mid, sem.at[0, n]).start()
+    for n, (src, mid, dst) in enumerate(pieces):
+        pltpu.make_async_copy(src, mid, sem.at[0, n]).wait()
+        pltpu.make_async_copy(mid, dst, sem.at[1, n]).start()
+    for n, (_, mid, dst) in enumerate(pieces):
+        pltpu.make_async_copy(mid, dst, sem.at[1, n]).wait()
 
 
 def per_device(nx, fields, buoyancy, stiffness, stress_zero, direct_effect, log_state, kernel, history, truncation):
@@ -559,24 +581,26 @@
         vm((NSTEP, 4 * nx, RB), F32),
         vm((rows, cols), F32),
         vm((rows, cols), F32),
-        vm((NSTEP, 2, planes, 8, cols), F32),
+        vm((NSTEP, 2, 8, cols), F32),
         vm((NSTEP, planes, rows, LW), F32),
         vm((NSTEP, rows, cols), F32),
-        vm((NSTEP, 2, planes, 8, cols), F32),
+        vm((NSTEP, 2, 8, cols), F32),
         vm((NSTEP, planes, rows, LW), F32),
+        vm((2, 2, 8, cols), F32),
         dma((21,)), dma((5 + NSTEP,)),
         dma((NSTEP,)), dma((NSTEP,)), dma((NSTEP,)), dma((NSTEP,)),
         dma((2, NSTEP)), dma((2, NSTEP)), dma((2, NSTEP)), dma((2, NSTEP)),
         dma((3,)), dma((3, NSTEP)), dma((3,)), dma((3, NSTEP)), dma, dma((NSTEP,)),
     ]
     hbm = pl.BlockSpec(memory_space=pl.ANY)
-    out_f, out_l, out_s = pl.pallas_call(
+    out_shape = (
+        jax.ShapeDtypeStruct((4, planes, rows, cols), F32),
+        jax.ShapeDtypeStruct((rows, cols), F32),
+        jax.ShapeDtypeStruct((NSTEP, 2 * RB, A), F32),
+    )
+    results = pl.pallas_call(
         functools.partial(kernel_body, nx),
-        out_shape=(
-            jax.ShapeDtypeStruct((4, planes, rows, cols), F32),
-            jax.ShapeDtypeStruct((rows, cols), F32),
-            jax.ShapeDtypeStruct((NSTEP, 2 * RB, A), F32),
-        ),
+        out_shape=out_shape,
         in_specs=[hbm] * len(args),
         out_specs=(hbm, hbm, hbm),
         scratch_shapes=scratch,
@@ -584,6 +608,14 @@
             collective_id=0, has_side_effects=True, vmem_limit_bytes=60 * 1024 * 1024
         ),
     )(*args)
+    out_f, out_l, out_s = pl.pallas_call(
+        hand_over,
+        out_shape=out_shape,
+        in_specs=[hbm] * 3,
+        out_specs=(hbm, hbm, hbm),
+        scratch_shapes=[vm(x.shape, F32) for x in out_shape] + [dma((2, 6))],
+        compiler_params=pltpu.CompilerParams(vmem_limit_bytes=60 * 1024 * 1024),
+    )(*results)
     spectra = out_s.reshape(NSTEP, modes, B, 2, A).transpose(0, 1, 3, 2, 4).reshape(NSTEP, modes, 2, strike)
     return out_f.reshape(4, 1, planes, rows, cols), out_l, spectra
 

time: 116 us -> 106 us (0.914)
  Pallas kernels: 111 us -> 105 us
  local copies, waits for them, and re-layouts: 4.66 us -> 0 us
    pallas_call x1 -> x2, Pallas kernels: 111 us -> 105 us  [the longest x1 102 us: per_device(): pl.pallas_call(functools.partial(kernel_body, nx), out_shape=out_shape, i...]
    unnamed x7 -> x0, local copies, waits for them, and re-layouts: 4.66 us -> none
where the time goes in v3:
time: 106 us
  Pallas kernels  105 us (99%)
    pallas_call x1, Pallas kernels, per_device(): pl.pallas_call(functools.partial(kernel_body, nx), out_shape=out_shape, i...  102 us
    pallas_call x1, Pallas kernels, per_device(): pl.pallas_call(hand_over, out_shape=out_shape, in_specs=[hbm] * 3, out_sp...  2.66 us

profile of v3, /device:TPU:1, one launch (start us, length us, event | category | flops | bytes accessed | tf_op | source)
XLA Modules:
  0.0 105.8 jit_solution(7606992160637167377)
XLA Ops:
  0.6 102.5 %shard_map.193 = (f32[4,4,64,512]{3,2,1,0:T(8,128)}, f32[64,512]{1,0:T(8,128)}, f32[4,256,128]{2,1,0:T(8,128)}) custom-call(f32[4,4,64,512]{3,2,1,0:T(8,128)} %bitcast.26, f32[4,64,512]{2,1,0:T(8,128)} %bitcast.29, f32[4,64,512]{2,1,0:T(8,128)} %bitcast.30, f32[64,512]{1,0:T(8,128)} %szero_h.1, f32[64,512]{1,0:T(8,128)} %direct_h.1, f32[64,512]{1,0:T(8,128)} %logs_h.1, ...), custom_call_target="tpu_custom_call" | custom-call | tf_op jit(solution)/shard_map/pallas_call | solution.py:601
  103.1 2.7 %shard_map.194 = (f32[4,4,64,512]{3,2,1,0:T(8,128)}, f32[64,512]{1,0:T(8,128)}, f32[4,256,128]{2,1,0:T(8,128)}) custom-call(f32[4,4,64,512]{3,2,1,0:T(8,128)} %get-tuple-element.9.f_in, f32[64,512]{1,0:T(8,128)} %get-tuple-element.10.l_in, f32[4,256,128]{2,1,0:T(8,128)} %get-tuple-element.11.s_in), custom_call_target="tpu_custom_call" | custom-call | tf_op jit(solution)/shard_map/pallas_call | solution.py:611

commit v4 on v3

--- a/solution.py
+++ b/solution.py
@@ -26,6 +26,10 @@
 
 def cis(turns):
     return np.cos(2 * np.pi * turns), np.sin(2 * np.pi * turns)
+
+
+def x_layers(nx):
+    return 4 if nx == 64 else nx
 
 
 def make_tables(nx, rows, modes, scale):
@@ -53,7 +57,9 @@
     c, s = cis(np.outer(i, z) / A)
     sign = np.where(np.arange(2)[:, None] * z[None, :] % 2 == 1, -1.0, 1.0)
     inv = np.array([[c, -s], [s, c]])
-    TI = np.einsum("xyiz,gz,pn->giypnxz", inv, sign, eye_p).reshape(8 * nx, 4 * A)
+    layers = x_layers(nx)
+    TI = np.einsum("xyiz,gz,pn->giypnxz", inv, sign, eye_p).reshape(2, layers, 4 * nx // layers, 4 * A)
+    TI = TI.transpose(1, 0, 2, 3).reshape(8 * nx, 4 * A)
     fwd = np.array([[c, s], [-s, c]])
     TF = np.einsum("xyiz,pn->ipxnyz", fwd, eye_p).reshape(4 * nx, 4 * A)
     zz = np.arange(depth).reshape(2 * R, 1, A)
@@ -114,41 +120,33 @@
     rows_in = pl.ds(8, RW)
     cols_in = pl.ds(LW, CW)
 
+    LX = x_layers(nx)
+    ZY = nx // LX
+    jx = lax.div(j, ZY)
     if nx == 64:
         turn = (2, 3, 1, 0)
-        xs = [lax.rem(lax.div(j, 16) + k, 4) * 16 for k in turn]
-        ys = [lax.rem(j, 4) + k for k in turn]
-        peers_xy = [x + lax.rem(y, 4) for x in xs for y in ys]
-        zs = lax.rem(lax.div(j, 4), 4)
-        outer = 4
-
-        def layer(i):
-            return lax.rem(zs + i + 2, 4) * 4
-
-        own_layer, own_xy = 2, 15
+        zs = [lax.rem(lax.div(j, 4) + k, 4) * 4 for k in turn]
+        ys = [lax.rem(j + k, 4) for k in turn]
+        inner = [z + y for y in ys for z in zs]
     else:
-        peers_xy = [j * 0]
-        outer = nx
-
-        def layer(i):
-            return lax.rem(j + i + 1, nx)
-
-        own_layer, own_xy = nx - 1, 0
+        inner = [j * 0]
 
     def each_peer(act):
         def one_layer(i, carry):
-            z = layer(i)
-            for n, xy in enumerate(peers_xy):
-                if n == own_xy:
-
-                    @pl.when(i != own_layer)
-                    def _():
-                        act(z + xy)
-                else:
-                    act(z + xy)
+            x = lax.rem(jx + i + LX // 2, LX) * ZY
+            for zy in inner[:-1]:
+                act(x + zy)
+
+            @pl.when(i != LX - LX // 2)
+            def _():
+                act(x + inner[-1])
+
             return carry
 
-        lax.fori_loop(0, outer, one_layer, 0)
+        lax.fori_loop(0, LX, one_layer, 0)
+
+    def layer_of(k):
+        return lax.rem(jx + LX - (LX // 2 + k) % LX, LX)
 
     barrier = pltpu.get_barrier_semaphore()
 
@@ -205,6 +203,14 @@
     for copy in loads[2:6]:
         copy.wait()
     lag_sums(0)
+
+    def strike_inverse(t):
+        x = table_left(L1, ACC[t], ((1,), (0,)))
+        xr, xi = x[:RB], x[RB:]
+        wide = jnp.concatenate([xr * TW[0] - xi * TW[1], xr * TW[1] + xi * TW[0]], axis=1)
+        GS[t] = table_left(T2, wide, ((1,), (1,)))
+
+    strike_inverse(0)
     loads[6].wait()
     pl.semaphore_wait(barrier, 2 * (nx - 1) + 2)
 
@@ -302,7 +308,6 @@
     pack_rows(0, VP, cols_in)
     first = v_copies(0)
     start_halo(*first[:4])
-    first[4].start()
 
     def out_copies():
         return [
@@ -314,21 +319,22 @@
         ]
 
     def step_body(t, carry):
-        x = table_left(L1, ACC[t], ((1,), (0,)))
-        xr, xi = x[:RB], x[RB:]
-        wide = jnp.concatenate([xr * TW[0] - xi * TW[1], xr * TW[1] + xi * TW[0]], axis=1)
-        GS[t] = table_left(T2, wide, ((1,), (1,)))
-        mine = pl.ds((g * nx + j) * 4, 4)
+        mine = pl.ds((jx * 2 * ZY + g * ZY + lax.rem(j, ZY)) * 4, 4)
+        landed = irecv.at[jx, t]
 
         def send_modes(peer):
             block = GS.at[t, pl.ds(peer * 4, 4)]
-            remote(block, RI.at[t, mine], isend.at[t], irecv.at[t], (1 - g, peer, q)).start()
-            remote(block, RI.at[t, mine], isend.at[t], irecv.at[t], (g, peer, q)).start()
+            remote(block, RI.at[t, mine], isend.at[t], landed, (1 - g, peer, q)).start()
+            remote(block, RI.at[t, mine], isend.at[t], landed, (g, peer, q)).start()
 
         each_peer(send_modes)
         own = GS.at[t, pl.ds(j * 4, 4)]
-        remote(own, RI.at[t, mine], isend.at[t], irecv.at[t], (1 - g, j, q)).start()
-        pltpu.make_async_copy(own, RI.at[t, mine], irecv.at[t]).start()
+        remote(own, RI.at[t, mine], isend.at[t], landed, (1 - g, j, q)).start()
+        pltpu.make_async_copy(own, RI.at[t, mine], landed).start()
+
+        @pl.when(t == 0)
+        def _():
+            first[4].start()
 
         @pl.when(t == 0)
         def _():
@@ -383,8 +389,18 @@
             for copy in loads[11:]:
                 copy.wait()
 
-        pltpu.make_async_copy(RI.at[t], RI.at[t], irecv.at[t]).wait()
-        OS[...] = table_right(RI[t].T, TI, ((1,), (0,)))
+        count = 8 * ZY
+        for k in range(0, LX, 2):
+            xs, spots = [], []
+            for n in (k, k + 1):
+                layer = layer_of(n)
+                spot = pl.ds(pl.multiple_of(layer * count, count), count)
+                pltpu.make_async_copy(RI.at[t, spot], RI.at[t, spot], irecv.at[layer, t]).wait()
+                xs.append(RI[t, spot, :].T)
+                spots.append(spot)
+            tab = [jnp.concatenate([TI[n, spot, :] for spot in spots], axis=0) for n in range(2)]
+            term = table_right(jnp.concatenate(xs, axis=1), tab, ((1,), (0,)))
+            OS[...] = term if k == 0 else OS[...] + term
 
         def depth_half(half, p, put):
             for hl in range(HC):
@@ -458,12 +474,13 @@
             depth_terms(1 - q, p, True)
         SF[t] = table_left(TF, US[...], ((1,), (1,)))
         spot = pl.ds(j * 4, 4)
+        arrived = frecv.at[jx, t]
 
         def send_slip(peer):
-            remote(SF.at[t, pl.ds(peer * 4, 4)], RF.at[t, spot], fsend.at[t], frecv.at[t], (g, peer, q)).start()
+            remote(SF.at[t, pl.ds(peer * 4, 4)], RF.at[t, spot], fsend.at[t], arrived, (g, peer, q)).start()
 
         each_peer(send_slip)
-        pltpu.make_async_copy(SF.at[t, spot], RF.at[t, spot], frecv.at[t]).start()
+        pltpu.make_async_copy(SF.at[t, spot], RF.at[t, spot], arrived).start()
 
         recv_halo(up, down, right, t, HS, DS, s_rows, d_cols)
         sent_halo(up, down, right, left)
@@ -507,15 +524,31 @@
         for p in range(2):
             parts[p].wait_send()
             slips[p].wait_send()
-        pltpu.make_async_copy(RF.at[t], RF.at[t], frecv.at[t]).wait()
-        x = table_right(RF[t].T, TV, ((1,), (0,)))
+        count = 4 * ZY
+        xs, spots = [], []
+        for k in range(0, LX, 2):
+            pair = []
+            for n in (k, k + 1):
+                layer = layer_of(n)
+                spot = pl.ds(pl.multiple_of(layer * count, count), count)
+                pltpu.make_async_copy(RF.at[t, spot], RF.at[t, spot], frecv.at[layer, t]).wait()
+                pair.append(RF[t, spot, :])
+                spots.append(spot)
+            xs.append(jnp.concatenate(pair, axis=0).T)
+        tab = [jnp.concatenate([TV[n, spot, :] for spot in spots], axis=0) for n in range(2)]
+        x = table_right(jnp.concatenate(xs, axis=1), tab, ((1,), (0,)))
         xr, xi = x[:, :A], x[:, A:]
         tall = jnp.concatenate([xr * TW[0] + xi * TW[1], xi * TW[0] - xr * TW[1]], axis=0)
         fresh = table_left(L3, tall, ((1,), (0,)))
         FR[t] = fresh
-        for d in range(NSTEP - 1):
-            ACC[t + 1 + d] = ACC[t + 1 + d] + WD[d] * fresh
         pltpu.make_async_copy(FR.at[t], out_s.at[t], outsem.at[5 + t]).start()
+
+        @pl.when(t < NSTEP - 1)
+        def _():
+            for d in range(NSTEP - 1):
+                ACC[t + 1 + d] = ACC[t + 1 + d] + WD[d] * fresh
+            strike_inverse(t + 1)
+
         return carry
 
     lax.fori_loop(0, NSTEP, step_body, 0)
@@ -588,7 +621,7 @@
         vm((NSTEP, planes, rows, LW), F32),
         vm((2, 2, 8, cols), F32),
         dma((21,)), dma((5 + NSTEP,)),
-        dma((NSTEP,)), dma((NSTEP,)), dma((NSTEP,)), dma((NSTEP,)),
+        dma((NSTEP,)), dma((x_layers(nx), NSTEP)), dma((NSTEP,)), dma((x_layers(nx), NSTEP)),
         dma((2, NSTEP)), dma((2, NSTEP)), dma((2, NSTEP)), dma((2, NSTEP)),
         dma((3,)), dma((3, NSTEP)), dma((3,)), dma((3, NSTEP)), dma, dma((NSTEP,)),
     ]

time: 106 us -> 107 us (level)
  no operation moved by 1% of the time
where the time goes in v4:
time: 107 us; the launch traced here: 106 us
  Pallas kernels  106 us (99%)
    pallas_call x1, Pallas kernels, per_device(): pl.pallas_call(functools.partial(kernel_body, nx), out_shape=out_shape, i...  103 us
    pallas_call x1, Pallas kernels, per_device(): pl.pallas_call(hand_over, out_shape=out_shape, in_specs=[hbm] * 3, out_sp...  2.66 us

profile of v4, /device:TPU:1, one launch (start us, length us, event | category | flops | bytes accessed | tf_op | source)
XLA Modules:
  0.0 106.3 jit_solution(16784793191563801437)
XLA Ops:
  0.6 103.0 %shard_map.193 = (f32[4,4,64,512]{3,2,1,0:T(8,128)}, f32[64,512]{1,0:T(8,128)}, f32[4,256,128]{2,1,0:T(8,128)}) custom-call(f32[4,4,64,512]{3,2,1,0:T(8,128)} %bitcast.26, f32[4,64,512]{2,1,0:T(8,128)} %bitcast.29, f32[4,64,512]{2,1,0:T(8,128)} %bitcast.30, f32[64,512]{1,0:T(8,128)} %szero_h.1, f32[64,512]{1,0:T(8,128)} %direct_h.1, f32[64,512]{1,0:T(8,128)} %logs_h.1, ...), custom_call_target="tpu_custom_call" | custom-call | tf_op jit(solution)/shard_map/pallas_call | solution.py:634
  103.7 2.7 %shard_map.194 = (f32[4,4,64,512]{3,2,1,0:T(8,128)}, f32[64,512]{1,0:T(8,128)}, f32[4,256,128]{2,1,0:T(8,128)}) custom-call(f32[4,4,64,512]{3,2,1,0:T(8,128)} %get-tuple-element.9.f_in, f32[64,512]{1,0:T(8,128)} %get-tuple-element.10.l_in, f32[4,256,128]{2,1,0:T(8,128)} %get-tuple-element.11.s_in), custom_call_target="tpu_custom_call" | custom-call | tf_op jit(solution)/shard_map/pallas_call | solution.py:644

commit v5 on v4

--- a/solution.py
+++ b/solution.py
@@ -30,6 +30,11 @@
 
 def x_layers(nx):
     return 4 if nx == 64 else nx
+
+
+def layer_order(nx):
+    places = np.arange(nx)
+    return places.reshape(4, 4, 4).transpose(1, 0, 2).reshape(nx) if nx == 64 else places
 
 
 def make_tables(nx, rows, modes, scale):
@@ -58,8 +63,10 @@
     sign = np.where(np.arange(2)[:, None] * z[None, :] % 2 == 1, -1.0, 1.0)
     inv = np.array([[c, -s], [s, c]])
     layers = x_layers(nx)
-    TI = np.einsum("xyiz,gz,pn->giypnxz", inv, sign, eye_p).reshape(2, layers, 4 * nx // layers, 4 * A)
-    TI = TI.transpose(1, 0, 2, 3).reshape(8 * nx, 4 * A)
+    TI = np.einsum("xyiz,gz,pn->giypnxz", inv, sign, eye_p).reshape(2, nx, 4, 4 * A)
+    by_layer = layer_order(nx)
+    TI = TI[:, by_layer].reshape(2, layers, 4 * nx // layers, 4 * A).transpose(1, 0, 2, 3).reshape(8 * nx, 4 * A)
+    TV = TV.reshape(nx, 4, 2 * A)[by_layer].reshape(4 * nx, 2 * A)
     fwd = np.array([[c, s], [-s, c]])
     TF = np.einsum("xyiz,pn->ipxnyz", fwd, eye_p).reshape(4 * nx, 4 * A)
     zz = np.arange(depth).reshape(2 * R, 1, A)
@@ -122,31 +129,32 @@
 
     LX = x_layers(nx)
     ZY = nx // LX
-    jx = lax.div(j, ZY)
     if nx == 64:
         turn = (2, 3, 1, 0)
-        zs = [lax.rem(lax.div(j, 4) + k, 4) * 4 for k in turn]
+        jz, step = lax.rem(lax.div(j, 4), 4), 4
+        jxy = lax.div(j, 16) * 4 + lax.rem(j, 4)
+        xs = [lax.rem(lax.div(j, 16) + k, 4) * 16 for k in turn]
         ys = [lax.rem(j + k, 4) for k in turn]
-        inner = [z + y for y in ys for z in zs]
+        inner = [x + y for x in xs for y in ys]
     else:
-        inner = [j * 0]
+        jz, step, jxy, inner = j, 1, j * 0, [j * 0]
 
     def each_peer(act):
         def one_layer(i, carry):
-            x = lax.rem(jx + i + LX // 2, LX) * ZY
-            for zy in inner[:-1]:
-                act(x + zy)
+            z = lax.rem(jz + i + LX // 2, LX) * step
+            for xy in inner[:-1]:
+                act(z + xy)
 
             @pl.when(i != LX - LX // 2)
             def _():
-                act(x + inner[-1])
+                act(z + inner[-1])
 
             return carry
 
         lax.fori_loop(0, LX, one_layer, 0)
 
     def layer_of(k):
-        return lax.rem(jx + LX - (LX // 2 + k) % LX, LX)
+        return lax.rem(jz + LX - (LX // 2 + k) % LX, LX)
 
     barrier = pltpu.get_barrier_semaphore()
 
@@ -319,8 +327,8 @@
         ]
 
     def step_body(t, carry):
-        mine = pl.ds((jx * 2 * ZY + g * ZY + lax.rem(j, ZY)) * 4, 4)
-        landed = irecv.at[jx, t]
+        mine = pl.ds((jz * 2 * ZY + g * ZY + jxy) * 4, 4)
+        landed = irecv.at[jz, t]
 
         def send_modes(peer):
             block = GS.at[t, pl.ds(peer * 4, 4)]
@@ -473,14 +481,15 @@
             pltpu.make_async_copy(land, land, lrecv.at[p, t]).wait()
             depth_terms(1 - q, p, True)
         SF[t] = table_left(TF, US[...], ((1,), (1,)))
-        spot = pl.ds(j * 4, 4)
-        arrived = frecv.at[jx, t]
+        spot = pl.ds((jz * ZY + jxy) * 4, 4)
+        block_here = pl.ds(j * 4, 4)
+        arrived = frecv.at[jz, t]
 
         def send_slip(peer):
             remote(SF.at[t, pl.ds(peer * 4, 4)], RF.at[t, spot], fsend.at[t], arrived, (g, peer, q)).start()
 
         each_peer(send_slip)
-        pltpu.make_async_copy(SF.at[t, spot], RF.at[t, spot], arrived).start()
+        pltpu.make_async_copy(SF.at[t, block_here], RF.at[t, spot], arrived).start()
 
         recv_halo(up, down, right, t, HS, DS, s_rows, d_cols)
         sent_halo(up, down, right, left)

time: 107 us -> 104 us (0.972)
  Pallas kernels: 106 us -> 103 us
    pallas_call x1, Pallas kernels: 103 us -> 101 us  [per_device(): pl.pallas_call(functools.partial(kernel_body, nx), out_shape=out_shape, i...]
where the time goes in v5:
time: 104 us
  Pallas kernels  103 us (99%)
    pallas_call x1, Pallas kernels, per_device(): pl.pallas_call(functools.partial(kernel_body, nx), out_shape=out_shape, i...  101 us
    pallas_call x1, Pallas kernels, per_device(): pl.pallas_call(hand_over, out_shape=out_shape, in_specs=[hbm] * 3, out_sp...  2.66 us

profile of v5, /device:TPU:1, one launch (start us, length us, event | category | flops | bytes accessed | tf_op | source)
XLA Modules:
  0.0 103.9 jit_solution(3238531987817941829)
XLA Ops:
  0.6 100.6 %shard_map.193 = (f32[4,4,64,512]{3,2,1,0:T(8,128)}, f32[64,512]{1,0:T(8,128)}, f32[4,256,128]{2,1,0:T(8,128)}) custom-call(f32[4,4,64,512]{3,2,1,0:T(8,128)} %bitcast.26, f32[4,64,512]{2,1,0:T(8,128)} %bitcast.29, f32[4,64,512]{2,1,0:T(8,128)} %bitcast.30, f32[64,512]{1,0:T(8,128)} %szero_h.1, f32[64,512]{1,0:T(8,128)} %direct_h.1, f32[64,512]{1,0:T(8,128)} %logs_h.1, ...), custom_call_target="tpu_custom_call" | custom-call | tf_op jit(solution)/shard_map/pallas_call | solution.py:643
  101.3 2.7 %shard_map.194 = (f32[4,4,64,512]{3,2,1,0:T(8,128)}, f32[64,512]{1,0:T(8,128)}, f32[4,256,128]{2,1,0:T(8,128)}) custom-call(f32[4,4,64,512]{3,2,1,0:T(8,128)} %get-tuple-element.9.f_in, f32[64,512]{1,0:T(8,128)} %get-tuple-element.10.l_in, f32[4,256,128]{2,1,0:T(8,128)} %get-tuple-element.11.s_in), custom_call_target="tpu_custom_call" | custom-call | tf_op jit(solution)/shard_map/pallas_call | solution.py:653

commit v6 on v5

--- a/solution.py
+++ b/solution.py
@@ -495,6 +495,33 @@
         sent_halo(up, down, right, left)
         NS[0] = TR[...]
 
+        def fault_chunk(i, c):
+            r0 = pl.multiple_of(i * 8, 8)
+            chunk = pl.ds(r0, 8)
+            inner = pl.ds(r0 + 8, 8)
+            n0, n1, n2, n3 = (NS[p, chunk, :] for p in range(4))
+            plane_terms = [
+                C1 * (n1 - n0) - C2 * n2,
+                C1 * (n2 - n1) - C2 * (n3 - n0),
+                C1 * (n3 - n2) + C2 * n1,
+                C2 * n2 - C1 * n3,
+            ]
+            for p in range(1):
+                tall = SP[p, pl.ds(r0, 24), :]
+                wide = DP[p, chunk, :]
+                dn1, dn2, up1 = (roll(tall, s, 0)[8:16] for s in (1, 2, -1))
+                total = plane_terms[p] + (C1 * (tall[8:16] - dn1) - C2 * (up1 - dn2))
+                dn1, dn2, up1 = (roll(wide, s, 1)[:, LW : LW + CW] for s in (1, 2, -1))
+                total = total + (C1 * (wide[:, LW : LW + CW] - dn1) - C2 * (up1 - dn2))
+                VP[p, inner, cols_in] = VP[p, inner, cols_in] + buoy[p, chunk, :] * total
+            return c
+
+        lax.fori_loop(0, RW // 8, fault_chunk, 0)
+
+        @pl.when(t < NSTEP - 1)
+        def _():
+            v_copies(t + 1)[4].start()
+
         def velocity_chunk(i, c):
             r0 = pl.multiple_of(i * 8, 8)
             chunk = pl.ds(r0, 8)
@@ -506,7 +533,7 @@
                 C1 * (n3 - n2) + C2 * n1,
                 C2 * n2 - C1 * n3,
             ]
-            for p in range(4):
+            for p in range(1, 4):
                 tall = SP[p, pl.ds(r0, 24), :]
                 wide = DP[p, chunk, :]
                 dn1, dn2, up1 = (roll(tall, s, 0)[8:16] for s in (1, 2, -1))
@@ -521,9 +548,7 @@
         @pl.when(t < NSTEP - 1)
         def _():
             pack_rows(0, VP, cols_in)
-            later = v_copies(t + 1)
-            start_halo(*later[:4])
-            later[4].start()
+            start_halo(*v_copies(t + 1)[:4])
 
         @pl.when(t == NSTEP - 1)
         def _():

time: 104 us -> 104 us (level)
  no operation moved by 1% of the time
where the time goes in v6:
time: 104 us
  Pallas kernels  103 us (99%)
    pallas_call x1, Pallas kernels, per_device(): pl.pallas_call(functools.partial(kernel_body, nx), out_shape=out_shape, i...  101 us
    pallas_call x1, Pallas kernels, per_device(): pl.pallas_call(hand_over, out_shape=out_shape, in_specs=[hbm] * 3, out_sp...  2.66 us

profile of v6, /device:TPU:1, one launch (start us, length us, event | category | flops | bytes accessed | tf_op | source)
XLA Modules:
  0.0 104.0 jit_solution(3957634268896809331)
XLA Ops:
  0.6 100.7 %shard_map.193 = (f32[4,4,64,512]{3,2,1,0:T(8,128)}, f32[64,512]{1,0:T(8,128)}, f32[4,256,128]{2,1,0:T(8,128)}) custom-call(f32[4,4,64,512]{3,2,1,0:T(8,128)} %bitcast.26, f32[4,64,512]{2,1,0:T(8,128)} %bitcast.29, f32[4,64,512]{2,1,0:T(8,128)} %bitcast.30, f32[64,512]{1,0:T(8,128)} %szero_h.1, f32[64,512]{1,0:T(8,128)} %direct_h.1, f32[64,512]{1,0:T(8,128)} %logs_h.1, ...), custom_call_target="tpu_custom_call" | custom-call | tf_op jit(solution)/shard_map/pallas_call | solution.py:668
  101.3 2.7 %shard_map.194 = (f32[4,4,64,512]{3,2,1,0:T(8,128)}, f32[64,512]{1,0:T(8,128)}, f32[4,256,128]{2,1,0:T(8,128)}) custom-call(f32[4,4,64,512]{3,2,1,0:T(8,128)} %get-tuple-element.9.f_in, f32[64,512]{1,0:T(8,128)} %get-tuple-element.10.l_in, f32[4,256,128]{2,1,0:T(8,128)} %get-tuple-element.11.s_in), custom_call_target="tpu_custom_call" | custom-call | tf_op jit(solution)/shard_map/pallas_call | solution.py:678

commit v7 on v6

--- a/solution.py
+++ b/solution.py
@@ -332,8 +332,8 @@
 
         def send_modes(peer):
             block = GS.at[t, pl.ds(peer * 4, 4)]
+            remote(block, RI.at[t, mine], isend.at[t], landed, (g, peer, q)).start()
             remote(block, RI.at[t, mine], isend.at[t], landed, (1 - g, peer, q)).start()
-            remote(block, RI.at[t, mine], isend.at[t], landed, (g, peer, q)).start()
 
         each_peer(send_modes)
         own = GS.at[t, pl.ds(j * 4, 4)]

time: 104 us -> 104 us (level)
  no operation moved by 1% of the time
where the time goes in v7:
time: 104 us; the launch traced here: 103 us
  Pallas kernels  103 us (99%)
    pallas_call x1, Pallas kernels, per_device(): pl.pallas_call(functools.partial(kernel_body, nx), out_shape=out_shape, i...  100 us
    pallas_call x1, Pallas kernels, per_device(): pl.pallas_call(hand_over, out_shape=out_shape, in_specs=[hbm] * 3, out_sp...  2.66 us

profile of v7, /device:TPU:1, one launch (start us, length us, event | category | flops | bytes accessed | tf_op | source)
XLA Modules:
  0.0 103.4 jit_solution(7501352295655443611)
XLA Ops:
  0.6 100.1 %shard_map.193 = (f32[4,4,64,512]{3,2,1,0:T(8,128)}, f32[64,512]{1,0:T(8,128)}, f32[4,256,128]{2,1,0:T(8,128)}) custom-call(f32[4,4,64,512]{3,2,1,0:T(8,128)} %bitcast.26, f32[4,64,512]{2,1,0:T(8,128)} %bitcast.29, f32[4,64,512]{2,1,0:T(8,128)} %bitcast.30, f32[64,512]{1,0:T(8,128)} %szero_h.1, f32[64,512]{1,0:T(8,128)} %direct_h.1, f32[64,512]{1,0:T(8,128)} %logs_h.1, ...), custom_call_target="tpu_custom_call" | custom-call | tf_op jit(solution)/shard_map/pallas_call | solution.py:668
  100.8 2.7 %shard_map.194 = (f32[4,4,64,512]{3,2,1,0:T(8,128)}, f32[64,512]{1,0:T(8,128)}, f32[4,256,128]{2,1,0:T(8,128)}) custom-call(f32[4,4,64,512]{3,2,1,0:T(8,128)} %get-tuple-element.9.f_in, f32[64,512]{1,0:T(8,128)} %get-tuple-element.10.l_in, f32[4,256,128]{2,1,0:T(8,128)} %get-tuple-element.11.s_in), custom_call_target="tpu_custom_call" | custom-call | tf_op jit(solution)/shard_map/pallas_call | solution.py:678
